TPU v7x, 512 devices: a whole 4x4x16 slice. The times are simulated.
512 devices in a mesh: src: 32 (over y, x, core), tgt: 16 (over z).
Axes of the slice: x: 4, y: 4, z: 16, core: 2. Of those that a mesh axis runs over, the one named last changes fastest.
Arguments:
- src_cells: float32 [50, 131072], P(None, ('src', 'tgt')), may hold values from -0.8 to 0.8
- tgt_cells: float32 [50, 8192], P(None, 'tgt'), may hold values from -0.8 to 0.8
- src_mass: float32 [131072], P('src'), may hold values from 0.5 to 2
- tgt_mass: float32 [8192], P('tgt'), may hold values from 0.5 to 2
Outputs:
- src_potential: float32 [131072], P('src')
- tgt_potential: float32 [8192], P('tgt')
All inputs are finite; a program needn't handle non-finite values.
Results may differ from a plain program's by a relative error of at most 0.00015.
Values sent between devices are 32-bit elements; how exact they have to be, the bound alone decides.
No kernel may reach another device: no remote copies, remote signals or barrier semaphores. Data moves between devices by JAX's collectives and lax.ppermute only.
A program may use at most 64 MiB of HBM per device.

v0:
```python
import jax
import jax.numpy as jnp
from jax import lax
from jax.sharding import PartitionSpec as P

ITERS = 2


epsilon_reg = 2.0


def gibbs_tile(src_block, tgt_block):
    src_norm = jnp.sum(src_block * src_block, axis=0)
    tgt_norm = jnp.sum(tgt_block * tgt_block, axis=0)
    cross = jnp.dot(
        src_block.T, tgt_block, precision=lax.Precision.HIGHEST, preferred_element_type=jnp.float32
    )
    cost = src_norm[:, None] + tgt_norm[None, :] - 2.0 * cross
    return jnp.exp(-cost / epsilon_reg)


def local(src_cells, tgt_cells, src_mass, tgt_mass):
    src_block = lax.all_gather(src_cells, "tgt", axis=1, tiled=True)
    stored_tile = gibbs_tile(src_block, tgt_cells)

    def get_tile():
        return stored_tile

    col_scale = jnp.ones((tgt_cells.shape[1],), jnp.float32)
    row_scale = jnp.ones((src_block.shape[1],), jnp.float32)
    for sweep in range(ITERS):
        row_part = jnp.dot(get_tile(), col_scale, precision=lax.Precision.HIGHEST)
        row_total = lax.psum(row_part, "tgt")
        row_scale = src_mass / row_total
        col_part = jnp.dot(row_scale, get_tile(), precision=lax.Precision.HIGHEST)
        col_total = lax.psum(col_part, "src")
        col_scale = tgt_mass / col_total
    return (epsilon_reg * jnp.log(row_scale), epsilon_reg * jnp.log(col_scale))


def solution(mesh):
    placed = (P(None, ("src", "tgt")), P(None, "tgt"), P("src"), P("tgt"))
    return jax.shard_map(
        local, mesh=mesh, in_specs=placed, out_specs=(P("src"), P("tgt")), check_vma=False
    )
```

profile of v0, /device:TPU:1, one launch (start us, length us, event | category | flops | bytes accessed | tf_op | source)
XLA Modules:
  0.0 317.8 jit_solution(1861517863350990255)
XLA Ops:
  0.6 0.9 multiply_reduce_fusion.1
  1.6 34.9 %all_gather.3 = f32[50,4096]{1,0:T(8,128)S(1)} all-gather(f32[50,256]{1,0:T(8,128)} %param.4), channel_id=1, replica_groups=mesh['src'=32,'tgt'=16] {'tgt'}, dimensions={1}, use_global_device_ids=true | all-gather | bytes 870400 | tf_op jit(solution)/shard_map/all_gather | solution.py:23
  36.4 0.1 multiply_reduce_fusion
  36.5 9.2 %multiply_exponential_fusion = f32[4096,512]{1,0:T(8,128)S(1)} fusion(f32[50,4096]{1,0:T(8,128)S(1)} %all_gather.3, f32[50,512]{1,0:T(8,128)} %param.5, f32[512]{0:T(512)S(1)} %multiply_reduce_fusion.1, f32[4096]{0:T(1024)S(1)} %multiply_reduce_fusion), kind=kOutput, calls=%fused_computation | convolution fusion | flops 1268776960 | bytes 9328640 | tf_op jit(solution)/shard_map/dot_general | solution.py:15
  45.7 0.0 copy-start
  45.7 3.2 %copy-done = f32[4096,512]{1,0:T(8,128)} copy-done((f32[4096,512]{1,0:T(8,128)}, f32[4096,512]{1,0:T(8,128)S(1)}, u32[]{:S(2)}) %copy-start) | copy-done | bytes 8388632
  48.9 0.0 copy-start.1
  48.9 0.0 copy-start.2
  48.9 7.3 %fusion = f32[1,4096]{1,0:T(1,128)S(1)} fusion(f32[4096,512]{1,0:T(8,128)S(1)} %multiply_exponential_fusion), kind=kOutput, calls=%fused_computation.5 | convolution fusion | flops 25165824 | bytes 8404992 | tf_op jit(solution)/shard_map/dot_general | solution.py:32
  56.2 38.9 %psum.28 = f32[4096]{0:T(1024)S(1)} all-reduce(f32[4096]{0:T(1024)S(1)} %bitcast.18), channel_id=1, replica_groups=mesh['src'=32,'tgt'=16] {'tgt'}, use_global_device_ids=true, to_apply=%region_2.0 | all-reduce | flops 4096 | bytes 32768 | tf_op jit(solution)/shard_map/psum | solution.py:33
  95.1 0.0 copy-done.1
  95.1 6.4 %fusion.3 = f32[1,512]{1,0:T(1,128)S(1)} fusion(f32[4096,1]{0,1:T(1,128)S(1)} %bitcast.16, f32[4096,512]{1,0:T(8,128)} %copy-done), kind=kOutput, calls=%fused_computation.8 | convolution fusion | flops 25165824 | bytes 8407040 | tf_op jit(solution)/shard_map/dot_general | solution.py:35
  101.5 83.6 %psum.29 = f32[512]{0:T(512)S(1)} all-reduce(f32[512]{0:T(512)S(1)} %bitcast.22), channel_id=1, replica_groups=mesh['src'=32,'tgt'=16] {'src'}, use_global_device_ids=true, to_apply=%region_3.0 | all-reduce | flops 512 | bytes 4096 | tf_op jit(solution)/shard_map/psum | solution.py:36
  185.1 0.0 copy-done.2
  185.1 9.4 %fusion.4 = f32[1,4096]{1,0:T(1,128)S(1)} fusion(f32[4096,512]{1,0:T(8,128)} %copy-done, f32[512,1]{0,1:T(1,128)S(1)} %bitcast.20), kind=kOutput, calls=%fused_computation.9 | convolution fusion | flops 25165824 | bytes 8407040 | tf_op jit(solution)/shard_map/dot_general | solution.py:32
  194.6 39.5 %psum.30 = f32[4096]{0:T(1024)S(1)} all-reduce(f32[4096]{0:T(1024)S(1)} %bitcast.17), channel_id=1, replica_groups=mesh['src'=32,'tgt'=16] {'tgt'}, use_global_device_ids=true, to_apply=%region_4.0 | all-reduce | flops 4096 | bytes 32768 | tf_op jit(solution)/shard_map/psum | solution.py:33
  234.1 0.6 log_multiply_fusion
  234.7 6.4 %fusion.5 = f32[1,512]{1,0:T(1,128)S(1)} fusion(f32[4096,1]{0,1:T(1,128)S(1)} %bitcast.19, f32[4096,512]{1,0:T(8,128)} %copy-done), kind=kOutput, calls=%fused_computation.10 | convolution fusion | flops 25165824 | bytes 8407040 | tf_op jit(solution)/shard_map/dot_general | solution.py:35
  241.1 76.1 %psum.31 = f32[512]{0:T(512)S(1)} all-reduce(f32[512]{0:T(512)S(1)} %bitcast.21), channel_id=1, replica_groups=mesh['src'=32,'tgt'=16] {'src'}, use_global_device_ids=true, to_apply=%region_5.0 | all-reduce | flops 512 | bytes 4096 | tf_op jit(solution)/shard_map/psum | solution.py:36
  317.2 0.6 log_multiply_fusion.1
  (2 shorter events, 0.0 us)
Async XLA Ops:
  45.7 3.2 %copy-start = (f32[4096,512]{1,0:T(8,128)}, f32[4096,512]{1,0:T(8,128)S(1)}, u32[]{:S(2)}) copy-start(f32[4096,512]{1,0:T(8,128)S(1)} %multiply_exponential_fusion) | copy-start | bytes 25165828
  48.9 46.2 %copy-start.1 = (f32[4096]{0:T(1024)S(1)}, f32[4096]{0:T(1024)}, u32[]{:S(2)}) copy-start(f32[4096]{0:T(1024)} %param.6) | copy-start | bytes 49156
  48.9 136.2 %copy-start.2 = (f32[512]{0:T(512)S(1)}, f32[512]{0:T(512)}, u32[]{:S(2)}) copy-start(f32[512]{0:T(512)} %param.7) | copy-start | bytes 6148
where the time goes:
time: 318 us
  blocking collectives  273 us (86%)
  matrix products  38.6 us (12%)
  local copies, waits for them, and re-layouts  3.22 us (1%)
    psum x2, blocking collectives, local(): col_total = lax.psum(col_part, 'src')  160 us
    psum x2, blocking collectives, local(): row_total = lax.psum(row_part, 'tgt')  78.5 us
    all_gather x1, blocking collectives, local(): src_block = lax.all_gather(src_cells, 'tgt', axis=1, tiled=True)  34.9 us
    dot_general x2, matrix products, local(): row_part = jnp.dot(get_tile(), col_scale, precision=lax.Precision.HIGHEST)  16.7 us
    dot_general x2, matrix products, local(): col_part = jnp.dot(row_scale, get_tile(), precision=lax.Precision.HIGHEST)  12.7 us
    dot_general x1, matrix products, gibbs_tile(): jnp.dot(src_block.T, tgt_block, precision=lax.Precision.HIGHEST, preferre...  9.15 us

commit v1 on v0

v1 whole, which is shorter than its diff:
```python
import jax
import jax.numpy as jnp
from jax import lax
from jax.experimental import pallas as pl
from jax.experimental.pallas import tpu as pltpu
from jax.sharding import Mesh, PartitionSpec as P

NY, NX, NC, NZ = 4, 4, 2, 16
NG = NX * NC
PLANE = ("y", "x", "core")
GROUP = ("x", "core")
PC = 50
HALF = 26
MASS = 56
ROWS, COLS = 2048, 1024
PIECE = 64
OWN = 256
EPS = 2.0


def split(value):
    high = value.astype(jnp.bfloat16)
    low = (value - high.astype(jnp.float32)).astype(jnp.bfloat16)
    return high, low


def pieces(norm):
    first = norm.astype(jnp.bfloat16).astype(jnp.float32)
    rest = norm - first
    second = rest.astype(jnp.bfloat16).astype(jnp.float32)
    return first, second, rest - second


def masked(cells):
    row = lax.broadcasted_iota(jnp.int32, cells.shape, 0)
    keep = (row < HALF) | ((row >= 32) & (row < 32 + PC - HALF))
    return row, jnp.where(keep, cells, 0.0)


def gibbs_kernel(rows_ref, cols_ref, gibbs_ref, part_ref, row_mass_ref, col_mass_ref, x_ref, y_ref):
    for g in range(NG):
        here = slice(g * OWN, (g + 1) * OWN)
        cells = rows_ref[g]
        row_mass_ref[:, here] = cells[MASS : MASS + 1]
        row, cells = masked(cells)
        first, second, third = pieces(-0.5 * jnp.sum(cells * cells, axis=0, keepdims=True))
        high, low = split(cells)
        extra = jnp.where(row == 26, first, jnp.where(row == 27, second, jnp.where(row == 28, third, 0.0)))
        extra = jnp.where((row >= 29) & (row < 32), 1.0, extra)
        x_ref[0:64, here] = (high.astype(jnp.float32) + extra).astype(jnp.bfloat16)
        x_ref[64:128, here] = high
        x_ref[128:192, here] = low
        x_ref[192:256, here] = low
    lane = lax.broadcasted_iota(jnp.int32, (32, 128), 1)
    for t in range(NZ // 2):
        here = slice(t * 128, (t + 1) * 128)
        a, b = cols_ref[2 * t], cols_ref[2 * t + 1]
        top = jnp.where(lane < 64, a, pltpu.roll(b, 64, 1))
        bottom = jnp.where(lane < 64, pltpu.roll(a, 64, 1), b)
        col_mass_ref[:, here] = bottom[MASS - 32 : MASS - 31]
        row, cells = masked(jnp.concatenate([top, bottom], axis=0))
        first, second, third = pieces(-0.5 * jnp.sum(cells * cells, axis=0, keepdims=True))
        high, low = split(cells)
        extra = jnp.where(row == 29, first, jnp.where(row == 30, second, jnp.where(row == 31, third, 0.0)))
        extra = jnp.where((row >= 26) & (row < 29), 1.0, extra)
        both = jnp.concatenate([high.astype(jnp.float32) + extra, low.astype(jnp.float32)], axis=0)
        turned = both.T.astype(jnp.bfloat16)
        y_ref[here, 0:128] = turned
        y_ref[here, 128:256] = turned
    for n in range(ROWS // 256):
        there = slice(n * 256, (n + 1) * 256)
        total = jnp.zeros((8, 256), jnp.float32)
        for m in range(COLS // 256):
            here = slice(m * 256, (m + 1) * 256)
            tile = jnp.exp(jnp.dot(y_ref[here, :], x_ref[:, there], preferred_element_type=jnp.float32))
            gibbs_ref[here, there] = tile
            total = total + jnp.sum(tile.reshape(32, 8, 256), axis=0)
        part_ref[:, there] = jnp.sum(total, axis=0, keepdims=True)


def column_kernel(gibbs_ref, parts_ref, mass_ref, part_ref, scale_ref):
    scale_ref[...] = mass_ref[...] / jnp.sum(parts_ref[...], axis=0, keepdims=True)
    for j in range(COLS // 128):
        here = slice(j * 128, (j + 1) * 128)
        total = jnp.zeros((128, 128), jnp.float32)
        for i in range(ROWS // 128):
            there = slice(i * 128, (i + 1) * 128)
            total = total + gibbs_ref[here, there] * scale_ref[:, there]
        part_ref[:, here] = jnp.sum(total.T, axis=0, keepdims=True)


def row_kernel(gibbs_ref, parts_ref, mass_ref, part_ref):
    scale = mass_ref[...] / jnp.sum(parts_ref[...], axis=0, keepdims=True)
    totals = [jnp.zeros((8, 128), jnp.float32)] * (ROWS // 128)
    for j in range(COLS // 128):
        here = slice(j * 128, (j + 1) * 128)
        spread = jnp.broadcast_to(scale[:, here], (128, 128)).T
        for i in range(ROWS // 128):
            there = slice(i * 128, (i + 1) * 128)
            totals[i] = totals[i] + jnp.sum((gibbs_ref[here, there] * spread).reshape(16, 8, 128), axis=0)
    for i in range(ROWS // 128):
        part_ref[:, i * 128 : (i + 1) * 128] = jnp.sum(totals[i], axis=0, keepdims=True)


def f32(*shape):
    return jax.ShapeDtypeStruct(shape, jnp.float32)


def call(kernel, outs, *args, scratch=()):
    whole = pl.BlockSpec(memory_space=pltpu.VMEM)
    return pl.pallas_call(
        kernel,
        out_shape=outs,
        in_specs=[whole] * len(args),
        out_specs=[whole] * len(outs),
        scratch_shapes=list(scratch),
        compiler_params=pltpu.CompilerParams(vmem_limit_bytes=24 << 20),
    )(*args)


def swap(value, axes):
    return lax.all_to_all(value, axes, 0, 0, tiled=True)


def gather(value, axes, count):
    return swap(jnp.broadcast_to(value[None], (count,) + value.shape), axes)


def local(src_cells, tgt_cells, src_mass, tgt_mass):
    me = lax.axis_index("x") * NC + lax.axis_index("core")
    own_mass = lax.dynamic_slice(src_mass, (lax.axis_index("z") * OWN,), (OWN,))
    gap = jnp.zeros((6, OWN), jnp.float32)
    rows = jnp.concatenate(
        [src_cells[:HALF], gap, src_cells[HALF:], own_mass[None], gap, gap[:1]], axis=0
    )
    piece = lax.dynamic_slice(tgt_cells, (0, me * PIECE), (PC, PIECE))
    piece_mass = lax.dynamic_slice(tgt_mass, (me * PIECE,), (PIECE,))
    bottom = jnp.concatenate([piece[HALF:], piece_mass[None], jnp.zeros((1, PIECE), jnp.float32)], axis=0)
    cols = jnp.concatenate([piece[:HALF], bottom], axis=1)
    cols = gather(cols.reshape(HALF * 128), "z", NZ).reshape(NZ, HALF, 128)
    cols = jnp.pad(cols, ((0, 0), (0, 32 - HALF), (0, 0)))
    rows = gather(rows, GROUP, NG)

    gibbs, row_part, row_mass, col_mass = call(
        gibbs_kernel,
        (f32(COLS, ROWS), f32(1, ROWS), f32(1, ROWS), f32(1, COLS)),
        rows,
        cols,
        scratch=(pltpu.VMEM((256, ROWS), jnp.bfloat16), pltpu.VMEM((COLS, 256), jnp.bfloat16)),
    )
    outs = (f32(1, COLS), f32(1, ROWS))
    row_parts = gather(row_part[0], GROUP, NG)
    col_part, _ = call(column_kernel, outs, gibbs, row_parts, row_mass)
    col_part = jnp.sum(gather(col_part[0], "y", NY), axis=0)
    col_parts = gather(col_part, "z", NZ)
    (row_part,) = call(row_kernel, (f32(1, ROWS),), gibbs, col_parts, col_mass)
    row_parts = gather(row_part[0], GROUP, NG)
    col_part, row_scale = call(column_kernel, outs, gibbs, row_parts, row_mass)

    own_scale = lax.dynamic_slice(row_scale[0], (me * OWN,), (OWN,))
    leaving = jnp.concatenate(
        [col_part.reshape(NZ, PIECE), jnp.broadcast_to(own_scale[None], (NZ, OWN))], axis=1
    )
    landed = swap(leaving, "z")
    row_out = EPS * jnp.log(landed[:, PIECE:].reshape(NZ * OWN))
    col_part = gather(jnp.sum(landed[:, :PIECE], axis=0), PLANE, NY * NG)
    col_total = jnp.sum(col_part.reshape(NY, NG * PIECE), axis=0)
    return row_out, EPS * jnp.log(tgt_mass / col_total)


def solution(mesh):
    grid = Mesh(mesh.devices.reshape(NY, NX, NC, NZ), ("y", "x", "core", "z"))
    placed = (P(None, PLANE + ("z",)), P(None, "z"), P(PLANE), P("z"))
    return jax.shard_map(local, mesh=grid, in_specs=placed, out_specs=(P(PLANE), P("z")), check_vma=False)
```

time: 318 us -> 142 us (0.45)
  blocking collectives: 273 us -> 46.4 us
  matrix products: 38.6 us -> 0 us
  starting transfers between devices: 0 us -> 38 us
  waiting for transfers between devices: 0 us -> 30.4 us
  local copies, waits for them, and re-layouts: 3.22 us -> 19.1 us
  Pallas kernels: 0 us -> 4.06 us
    psum x4 -> x0, blocking collectives: 238 us -> none  [the longest x2 160 us: local(): col_total = lax.psum(col_part, 'src')]
    all_to_all x0 -> x4, blocking collectives: none -> 46.4 us  [swap(): return lax.all_to_all(value, axes, 0, 0, tiled=True)]
    dot_general x5 -> x0, matrix products: 38.6 us -> none  [the longest x2 16.7 us: local(): row_part = jnp.dot(get_tile(), col_scale, precision=lax.Precision.HIGHEST)]
    all_to_all x0 -> x4, starting transfers between devices: none -> 38 us  [swap(): return lax.all_to_all(value, axes, 0, 0, tiled=True)]
    all_gather x1 -> x0, blocking collectives: 34.9 us -> none  [local(): src_block = lax.all_gather(src_cells, 'tgt', axis=1, tiled=True)]
    all_to_all x0 -> x4, waiting for transfers between devices: none -> 30.4 us  [swap(): return lax.all_to_all(value, axes, 0, 0, tiled=True)]
    unnamed x6 -> x13, local copies, waits for them, and re-layouts: 3.22 us -> 10.7 us
    pallas_call x0 -> x4, Pallas kernels: none -> 4.06 us  [call(): pl.pallas_call(kernel, out_shape=outs, in_specs=[whole] * len(args), out_...]
  transfers between devices with their start and end apart: 0 -> 4, of which waited for: 0 -> 4; matrix products, arithmetic and copies ran while one was open for 0% -> 3% of each run, Pallas kernels for 0% -> 0%
where the time goes in v1:
time: 142 us; the launch traced here: 141 us
  blocking collectives  46.4 us (33%)
  starting transfers between devices  38 us (27%)
  waiting for transfers between devices  30.4 us (21%)
  local copies, waits for them, and re-layouts  19.1 us (13%)
  Pallas kernels  4.06 us (3%)
  other arithmetic  2.67 us (2%)
    all_to_all x4, blocking collectives, swap(): return lax.all_to_all(value, axes, 0, 0, tiled=True)  46.4 us
    all_to_all x4, starting transfers between devices, swap(): return lax.all_to_all(value, axes, 0, 0, tiled=True)  38 us
    all_to_all x4, waiting for transfers between devices, swap(): return lax.all_to_all(value, axes, 0, 0, tiled=True)  30.4 us
    unnamed x13, local copies, waits for them, and re-layouts  10.7 us
    pallas_call x4, Pallas kernels, call(): pl.pallas_call(kernel, out_shape=outs, in_specs=[whole] * len(args), out_...  4.06 us
    broadcast_in_dim x7, local copies, waits for them, and re-layouts, gather(): return swap(jnp.broadcast_to(value[None], (count,) + value.shape), axes)  2.97 us
  transfers between devices with their start and end apart: 4, of which 4 were waited for; matrix products, arithmetic and copies ran while one was open for 3% of the time, Pallas kernels for 0%

profile of v1, /device:TPU:1, one launch (start us, length us, event | category | flops | bytes accessed | tf_op | source)
XLA Modules:
  0.0 141.4 jit_solution(5479566888249066315)
XLA Ops:
  0.6 0.8 constant_dynamic-slice_fusion
  1.4 0.8 dynamic-slice.2
  3.1 0.8 broadcast_in_dim.66
  3.8 15.7 %all-to-all-start.1 = ((f32[16,1,3328]{2,1,0:T(1,128)}), f32[16,1,3328]{2,1,0:T(1,128)S(1)}, u32[]{:S(2)}, u32[]{:S(2)}) async-start(f32[16,1,3328]{2,1,0:T(1,128)} %broadcast_in_dim.66), calls=%async_computation.1 | async-start | bytes 425984 | tf_op jit(solution)/shard_map/all_to_all | solution.py:122
  19.6 0.8 slice.21
  20.4 0.8 slice.22
  21.1 0.8 dynamic_slice.12
  21.9 10.3 %all-to-all-done.1 = f32[16,1,3328]{2,1,0:T(1,128)S(1)} async-done(((f32[16,1,3328]{2,1,0:T(1,128)}), f32[16,1,3328]{2,1,0:T(1,128)S(1)}, u32[]{:S(2)}, u32[]{:S(2)}) %all-to-all-start.1) | async-done | bytes 213024 | tf_op jit(solution)/shard_map/all_to_all | solution.py:122
  32.2 0.8 broadcast_in_dim.30
  33.0 9.6 %all-to-all-start = ((f32[8,64,256]{2,1,0:T(8,128)}), f32[8,64,256]{2,1,0:T(8,128)S(1)}, u32[]{:S(2)}, u32[]{:S(2)}) async-start(f32[8,64,256]{2,1,0:T(8,128)} %broadcast_in_dim.30), calls=%async_computation | async-start | bytes 1048576 | tf_op jit(solution)/shard_map/all_to_all | solution.py:122
  43.2 8.9 %all-to-all-done.rows_ref = f32[8,64,256]{2,1,0:T(8,128)S(1)} async-done(((f32[8,64,256]{2,1,0:T(8,128)}), f32[8,64,256]{2,1,0:T(8,128)S(1)}, u32[]{:S(2)}, u32[]{:S(2)}) %all-to-all-start) | async-done | bytes 524320 | tf_op jit(solution)/shard_map/all_to_all | solution.py:122
  52.1 1.5 %shard_map.59 = (f32[1024,2048]{1,0:T(8,128)S(1)}, f32[1,2048]{1,0:T(1,128)S(1)}, f32[1,2048]{1,0:T(1,128)S(1)}, f32[1,1024]{1,0:T(1,128)S(1)}) custom-call(f32[8,64,256]{2,1,0:T(8,128)S(1)} %all-to-all-done.rows_ref, f32[16,32,128]{2,1,0:T(8,128)S(1)} %pad.4.cols_ref), custom_call_target="tpu_custom_call" | custom-call | tf_op jit(solution)/shard_map/pallas_call | solution.py:111
  53.7 8.1 %all_to_all.59 = f32[8,1,2048]{2,1,0:T(1,128)S(1)} all-to-all(f32[8,1,2048]{2,1,0:T(1,128)S(1)} %broadcast_in_dim.67), channel_id=1, replica_groups=mesh['y'=4,'x'=4,'core'=2,'z'=16] {'x','core'}, dimensions={0} | all-to-all | bytes 131072 | tf_op jit(solution)/shard_map/all_to_all | solution.py:122
  61.8 1.2 shard_map.60
  63.0 3.2 %copy-done = f32[1024,2048]{1,0:T(8,128)} copy-done((f32[1024,2048]{1,0:T(8,128)}, f32[1024,2048]{1,0:T(8,128)S(1)}, u32[]{:S(2)}) %copy-start) | copy-done | bytes 8388632
  66.2 8.2 %all_to_all.60 = f32[4,1,1024]{2,1,0:T(1,128)S(1)} all-to-all(f32[4,1,1024]{2,1,0:T(1,128)S(1)} %broadcast_in_dim.68), channel_id=1, replica_groups=mesh['y'=4,'x'=4,'core'=2,'z'=16] {'y'}, dimensions={0} | all-to-all | bytes 32768 | tf_op jit(solution)/shard_map/all_to_all | solution.py:122
  74.5 16.3 %all_to_all.61 = f32[16,1,1024]{2,1,0:T(1,128)S(1)} all-to-all(f32[16,1,1024]{2,1,0:T(1,128)S(1)} %broadcast_in_dim.69), channel_id=1, replica_groups=mesh['y'=4,'x'=4,'core'=2,'z'=16] {'z'}, dimensions={0} | all-to-all | bytes 131072 | tf_op jit(solution)/shard_map/all_to_all | solution.py:122
  90.8 3.4 %copy-done.1 = f32[1024,2048]{1,0:T(8,128)S(1)} copy-done((f32[1024,2048]{1,0:T(8,128)S(1)}, f32[1024,2048]{1,0:T(8,128)}, u32[]{:S(2)}) %copy-start.1) | copy-done | bytes 8388632
  95.5 7.0 %all-to-all-start.5 = ((f32[8,1,2048]{2,1,0:T(1,128)}), f32[8,1,2048]{2,1,0:T(1,128)S(1)}, u32[]{:S(2)}, u32[]{:S(2)}) async-start(f32[8,1,2048]{2,1,0:T(1,128)} %broadcast_in_dim.70), calls=%async_computation.5 | async-start | bytes 131072 | tf_op jit(solution)/shard_map/all_to_all | solution.py:122
  102.5 4.9 %all-to-all-done.5 = f32[8,1,2048]{2,1,0:T(1,128)S(1)} async-done(((f32[8,1,2048]{2,1,0:T(1,128)}), f32[8,1,2048]{2,1,0:T(1,128)S(1)}, u32[]{:S(2)}, u32[]{:S(2)}) %all-to-all-start.5) | async-done | bytes 65568 | tf_op jit(solution)/shard_map/all_to_all | solution.py:122
  107.4 3.4 %copy-done.2 = f32[1024,2048]{1,0:T(8,128)S(1)} copy-done((f32[1024,2048]{1,0:T(8,128)S(1)}, f32[1024,2048]{1,0:T(8,128)}, u32[]{:S(2)}) %copy-start.2) | copy-done | bytes 8388632
  112.8 13.8 %all_to_all.62 = f32[16,1,320]{2,1,0:T(1,128)S(1)} all-to-all(f32[16,1,320]{2,1,0:T(1,128)S(1)} %all_to_all.47), channel_id=1, replica_groups=mesh['y'=4,'x'=4,'core'=2,'z'=16] {'z'}, dimensions={0} | all-to-all | bytes 40960 | tf_op jit(solution)/shard_map/all_to_all | solution.py:122
  127.3 5.7 %all-to-all-start.7 = ((f32[32,1,64]{2,1,0:T(1,128)}), f32[32,1,64]{2,1,0:T(1,128)S(1)}, u32[]{:S(2)}, u32[]{:S(2)}) async-start(f32[32,1,64]{2,1,0:T(1,128)} %broadcast_in_dim.73), calls=%async_computation.7 | async-start | bytes 32768 | tf_op jit(solution)/shard_map/all_to_all | solution.py:122
  133.7 6.4 %all-to-all-done.7 = f32[32,1,64]{2,1,0:T(1,128)S(1)} async-done(((f32[32,1,64]{2,1,0:T(1,128)}), f32[32,1,64]{2,1,0:T(1,128)S(1)}, u32[]{:S(2)}, u32[]{:S(2)}) %all-to-all-start.7) | async-done | bytes 8224 | tf_op jit(solution)/shard_map/all_to_all | solution.py:122
  (40 shorter events, 7.7 us)
Async XLA Ops:
  3.8 28.3 %all-to-all-start.1 = ((f32[16,1,3328]{2,1,0:T(1,128)}), f32[16,1,3328]{2,1,0:T(1,128)S(1)}, u32[]{:S(2)}, u32[]{:S(2)}) async-start(f32[16,1,3328]{2,1,0:T(1,128)} %broadcast_in_dim.66), calls=%async_computation.1 | async-start | bytes 425984 | tf_op jit(solution)/shard_map/all_to_all | solution.py:122
  33.0 19.1 %all-to-all-start = ((f32[8,64,256]{2,1,0:T(8,128)}), f32[8,64,256]{2,1,0:T(8,128)S(1)}, u32[]{:S(2)}, u32[]{:S(2)}) async-start(f32[8,64,256]{2,1,0:T(8,128)} %broadcast_in_dim.30), calls=%async_computation | async-start | bytes 1048576 | tf_op jit(solution)/shard_map/all_to_all | solution.py:122
  63.0 3.2 %copy-start = (f32[1024,2048]{1,0:T(8,128)}, f32[1024,2048]{1,0:T(8,128)S(1)}, u32[]{:S(2)}) copy-start(f32[1024,2048]{1,0:T(8,128)S(1)} %get-tuple-element.9.gibbs_ref) | copy-start | bytes 25165828
  90.8 3.4 %copy-start.1 = (f32[1024,2048]{1,0:T(8,128)S(1)}, f32[1024,2048]{1,0:T(8,128)}, u32[]{:S(2)}) copy-start(f32[1024,2048]{1,0:T(8,128)} %copy-done) | copy-start | bytes 25165828
  94.2 46.6 %copy-start.3 = (f32[512]{0:T(512)S(1)}, f32[512]{0:T(512)}, u32[]{:S(2)}) copy-start(f32[512]{0:T(512)} %param.7) | copy-start | bytes 6148
  95.5 11.8 %all-to-all-start.5 = ((f32[8,1,2048]{2,1,0:T(1,128)}), f32[8,1,2048]{2,1,0:T(1,128)S(1)}, u32[]{:S(2)}, u32[]{:S(2)}) async-start(f32[8,1,2048]{2,1,0:T(1,128)} %broadcast_in_dim.70), calls=%async_computation.5 | async-start | bytes 131072 | tf_op jit(solution)/shard_map/all_to_all | solution.py:122
  107.4 3.4 %copy-start.2 = (f32[1024,2048]{1,0:T(8,128)S(1)}, f32[1024,2048]{1,0:T(8,128)}, u32[]{:S(2)}) copy-start(f32[1024,2048]{1,0:T(8,128)} %copy-done) | copy-start | bytes 25165828
  127.3 12.7 %all-to-all-start.7 = ((f32[32,1,64]{2,1,0:T(1,128)}), f32[32,1,64]{2,1,0:T(1,128)S(1)}, u32[]{:S(2)}, u32[]{:S(2)}) async-start(f32[32,1,64]{2,1,0:T(1,128)} %broadcast_in_dim.73), calls=%async_computation.7 | async-start | bytes 32768 | tf_op jit(solution)/shard_map/all_to_all | solution.py:122

commit v2 on v1

v2 whole, which is shorter than its diff:
```python
import jax
import jax.numpy as jnp
from jax import lax
from jax.experimental import pallas as pl
from jax.experimental.pallas import tpu as pltpu
from jax.sharding import Mesh, PartitionSpec as P

NY, NX, NC, NZ = 4, 4, 2, 16
NG = NX * NC
PLANE = ("y", "x", "core")
GROUP = ("x", "core")
PC = 50
HALF = 26
MASS = 56
ROWS, COLS = 2048, 1024
PIECE = 64
OWN = 256
EPS = 2.0


def split(value):
    high = value.astype(jnp.bfloat16)
    low = (value - high.astype(jnp.float32)).astype(jnp.bfloat16)
    return high, low


def pieces(norm):
    first = norm.astype(jnp.bfloat16).astype(jnp.float32)
    rest = norm - first
    second = rest.astype(jnp.bfloat16).astype(jnp.float32)
    return first, second, rest - second


def masked(cells):
    row = lax.broadcasted_iota(jnp.int32, cells.shape, 0)
    keep = (row < HALF) | ((row >= 32) & (row < 32 + PC - HALF))
    return row, jnp.where(keep, cells, 0.0)


def pack_kernel(src_ref, tgt_ref, src_mass_ref, tgt_mass_ref, rows_ref, cols_ref):
    x, core, z = (lax.axis_index(name) for name in ("x", "core", "z"))
    rows_ref[...] = jnp.zeros_like(rows_ref)
    rows_ref[0:HALF] = src_ref[0:HALF]
    rows_ref[32 : 32 + PC - HALF] = src_ref[HALF:PC]
    for k in range(2):
        rows_ref[MASS : MASS + 1, k * 128 : (k + 1) * 128] = src_mass_ref[pl.ds(2 * z + k, 1)]
    here = pl.ds(pl.multiple_of(x * 128, 128), 128)
    cells = tgt_ref[:, here]
    top = cells[0:HALF]
    bottom = jnp.concatenate([cells[HALF:PC], tgt_mass_ref[pl.ds(x, 1)], jnp.zeros((1, 128), jnp.float32)], axis=0)
    lane = lax.broadcasted_iota(jnp.int32, (HALF, 128), 1)
    first = jnp.where(lane < PIECE, top, pltpu.roll(bottom, PIECE, 1))
    second = jnp.where(lane < PIECE, pltpu.roll(top, PIECE, 1), bottom)
    piece = jnp.where(jnp.broadcast_to(core, (HALF, 128)) == 0, first, second)
    for k in range(NZ):
        cols_ref[k * HALF : (k + 1) * HALF] = piece


def gibbs_kernel(own_ref, one_ref, two_ref, three_ref, cols_ref, gibbs_ref, part_ref, row_mass_ref, col_mass_ref, x_ref, y_ref):
    x = lax.axis_index("x")
    for k, rows_ref in enumerate((own_ref, one_ref, two_ref, three_ref)):
        base = pl.multiple_of(lax.rem(x + NX - k, NX) * (NC * OWN), NC * OWN)
        for c in range(NC):
            here = pl.ds(pl.multiple_of(base + c * OWN, OWN), OWN)
            cells = rows_ref[c]
            row_mass_ref[:, here] = cells[MASS : MASS + 1]
            row, cells = masked(cells)
            first, second, third = pieces(-0.5 * jnp.sum(cells * cells, axis=0, keepdims=True))
            high, low = split(cells)
            extra = jnp.where(row == 26, first, jnp.where(row == 27, second, jnp.where(row == 28, third, 0.0)))
            extra = jnp.where((row >= 29) & (row < 32), 1.0, extra)
            x_ref[0:64, here] = (high.astype(jnp.float32) + extra).astype(jnp.bfloat16)
            x_ref[64:128, here] = high
            x_ref[128:192, here] = low
            x_ref[192:256, here] = low
    lane = lax.broadcasted_iota(jnp.int32, (32, 128), 1)
    gap = jnp.zeros((32 - HALF, 128), jnp.float32)
    for t in range(NZ // 2):
        here = slice(t * 128, (t + 1) * 128)
        a, b = (
            jnp.concatenate([cols_ref[k * HALF : (k + 1) * HALF], gap], axis=0) for k in (2 * t, 2 * t + 1)
        )
        top = jnp.where(lane < PIECE, a, pltpu.roll(b, PIECE, 1))
        bottom = jnp.where(lane < PIECE, pltpu.roll(a, PIECE, 1), b)
        col_mass_ref[:, here] = bottom[MASS - 32 : MASS - 31]
        row, cells = masked(jnp.concatenate([top, bottom], axis=0))
        first, second, third = pieces(-0.5 * jnp.sum(cells * cells, axis=0, keepdims=True))
        high, low = split(cells)
        extra = jnp.where(row == 29, first, jnp.where(row == 30, second, jnp.where(row == 31, third, 0.0)))
        extra = jnp.where((row >= 26) & (row < 29), 1.0, extra)
        both = jnp.concatenate([high.astype(jnp.float32) + extra, low.astype(jnp.float32)], axis=0)
        turned = both.T.astype(jnp.bfloat16)
        y_ref[here, 0:128] = turned
        y_ref[here, 128:256] = turned
    for n in range(ROWS // 256):
        there = slice(n * 256, (n + 1) * 256)
        total = jnp.zeros((8, 256), jnp.float32)
        for m in range(COLS // 256):
            here = slice(m * 256, (m + 1) * 256)
            tile = jnp.exp(jnp.dot(y_ref[here, :], x_ref[:, there], preferred_element_type=jnp.float32))
            gibbs_ref[here, there] = tile
            total = total + jnp.sum(tile.reshape(32, 8, 256), axis=0)
        total = jnp.sum(total, axis=0, keepdims=True)
        for k in range(NG):
            part_ref[k, :, there] = total


def summed(parts_ref):
    total = parts_ref[0]
    for k in range(1, parts_ref.shape[0]):
        total = total + parts_ref[k]
    return total


def columns(gibbs_ref, scale_ref, j):
    here = slice(j * 128, (j + 1) * 128)
    total = jnp.zeros((128, 128), jnp.float32)
    for i in range(ROWS // 128):
        there = slice(i * 128, (i + 1) * 128)
        total = total + gibbs_ref[here, there] * scale_ref[:, there]
    return jnp.sum(total.T, axis=0, keepdims=True)


def column_kernel(gibbs_ref, parts_ref, mass_ref, part_ref, scale_ref):
    scale_ref[...] = mass_ref[...] / summed(parts_ref)
    for j in range(COLS // 128):
        total = columns(gibbs_ref, scale_ref, j)
        for k in range(NY):
            part_ref[k, :, j * 128 : (j + 1) * 128] = total


def relay_kernel(parts_ref, part_ref):
    total = summed(parts_ref)
    for k in range(part_ref.shape[0]):
        part_ref[k] = total


def last_column_kernel(gibbs_ref, parts_ref, mass_ref, leaving_ref, scale_ref):
    scale_ref[...] = mass_ref[...] / summed(parts_ref)
    me = lax.axis_index("x") * NC + lax.axis_index("core")
    own = scale_ref[:, pl.ds(pl.multiple_of(me * OWN, OWN), OWN)]
    for j in range(COLS // 128):
        total = columns(gibbs_ref, scale_ref, j)
        for k in (2 * j, 2 * j + 1):
            leaving_ref[k, :, 0:OWN] = own
            leaving_ref[k, :, OWN : OWN + 128] = total
            total = pltpu.roll(total, PIECE, 1)


def row_kernel(gibbs_ref, parts_ref, mass_ref, part_ref):
    scale = mass_ref[...] / summed(parts_ref)
    totals = [jnp.zeros((8, 128), jnp.float32)] * (ROWS // 128)
    for j in range(COLS // 128):
        here = slice(j * 128, (j + 1) * 128)
        spread = jnp.broadcast_to(scale[:, here], (128, 128)).T
        for i in range(ROWS // 128):
            there = slice(i * 128, (i + 1) * 128)
            totals[i] = totals[i] + jnp.sum((gibbs_ref[here, there] * spread).reshape(16, 8, 128), axis=0)
    for i in range(ROWS // 128):
        total = jnp.sum(totals[i], axis=0, keepdims=True)
        for k in range(NG):
            part_ref[k, :, i * 128 : (i + 1) * 128] = total


def landing_kernel(landed_ref, rows_ref, part_ref):
    total = jnp.zeros((1, 128), jnp.float32)
    for k in range(NZ):
        rows_ref[k] = EPS * jnp.log(landed_ref[k, :, 0:OWN])
        total = total + landed_ref[k, :, OWN : OWN + 128]
    for k in range(NY * NG):
        part_ref[k] = total


def potential_kernel(parts_ref, mass_ref, out_ref):
    lane = lax.broadcasted_iota(jnp.int32, (1, 128), 1)
    for t in range(NG // 2):
        a, b = (sum(parts_ref[y * NG + g] for y in range(NY)) for g in (2 * t, 2 * t + 1))
        total = jnp.where(lane < PIECE, a, pltpu.roll(b, PIECE, 1))
        out_ref[t : t + 1] = EPS * jnp.log(mass_ref[t : t + 1] / total)


def f32(*shape):
    return jax.ShapeDtypeStruct(shape, jnp.float32)


def call(kernel, outs, *args, scratch=()):
    whole = pl.BlockSpec(memory_space=pltpu.VMEM)
    return pl.pallas_call(
        kernel,
        out_shape=outs,
        in_specs=[whole] * len(args),
        out_specs=[whole] * len(outs),
        scratch_shapes=list(scratch),
        compiler_params=pltpu.CompilerParams(vmem_limit_bytes=24 << 20),
    )(*args)


def swap(value, axes):
    return lax.all_to_all(value, axes, 0, 0, tiled=True)


def local(src_cells, tgt_cells, src_mass, tgt_mass):
    tgt_mass = tgt_mass.reshape(NX, 128)
    rows, cols = call(
        pack_kernel, (f32(64, OWN), f32(NZ * HALF, 128)), src_cells, tgt_cells, src_mass.reshape(NZ * 2, 128), tgt_mass
    )
    cols = swap(cols.reshape(NZ, 1, HALF * 128), "z").reshape(NZ * HALF, 128)
    rows = lax.all_gather(rows, "core")
    others = [lax.ppermute(rows, "x", [(i, (i + k) % NX) for i in range(NX)]) for k in range(1, NX)]
    gibbs, row_parts, row_mass, col_mass = call(
        gibbs_kernel,
        (f32(COLS, ROWS), f32(NG, 1, ROWS), f32(1, ROWS), f32(1, COLS)),
        rows,
        *others,
        cols,
        scratch=(pltpu.VMEM((256, ROWS), jnp.bfloat16), pltpu.VMEM((COLS, 256), jnp.bfloat16)),
    )
    scale = pltpu.VMEM((1, ROWS), jnp.float32)
    (col_parts,) = call(
        column_kernel, (f32(NY, 1, COLS),), gibbs, swap(row_parts, GROUP), row_mass, scratch=(scale,)
    )
    (col_parts,) = call(relay_kernel, (f32(NZ, 1, COLS),), swap(col_parts, "y"))
    col_parts = swap(col_parts, "z")
    (row_parts,) = call(row_kernel, (f32(NG, 1, ROWS),), gibbs, col_parts, col_mass)
    (leaving,) = call(
        last_column_kernel, (f32(NZ, 1, OWN + 128),), gibbs, swap(row_parts, GROUP), row_mass, scratch=(scale,)
    )
    row_out, col_parts = call(landing_kernel, (f32(NZ, 1, OWN), f32(NY * NG, 1, 128)), swap(leaving, "z"))
    (col_out,) = call(potential_kernel, (f32(NX, 128),), swap(col_parts, PLANE), tgt_mass)
    return row_out.reshape(NZ * OWN), col_out.reshape(NX * 128)


def solution(mesh):
    grid = Mesh(mesh.devices.reshape(NY, NX, NC, NZ), ("y", "x", "core", "z"))
    placed = (P(None, PLANE + ("z",)), P(None, "z"), P(PLANE), P("z"))
    return jax.shard_map(local, mesh=grid, in_specs=placed, out_specs=(P(PLANE), P("z")), check_vma=False)
```

time: 142 us -> 121 us (0.85)
  blocking collectives: 46.4 us -> 79.1 us
  waiting for transfers between devices: 30.4 us -> 6.15 us
  local copies, waits for them, and re-layouts: 19.1 us -> 3.11 us
  starting transfers between devices: 38 us -> 25.1 us
  other arithmetic: 2.67 us -> 0 us
  Pallas kernels: 4.06 us -> 5.84 us
    all_to_all x4 -> x1, waiting for transfers between devices: 30.4 us -> 0.01 us  [swap(): return lax.all_to_all(value, axes, 0, 0, tiled=True)]
    all_to_all x4 -> x6, blocking collectives: 46.4 us -> 76.6 us  [swap(): return lax.all_to_all(value, axes, 0, 0, tiled=True)]
    all_to_all x4 -> x1, starting transfers between devices: 38 us -> 15.7 us  [swap(): return lax.all_to_all(value, axes, 0, 0, tiled=True)]
    ppermute x0 -> x3, starting transfers between devices: none -> 9.32 us  [local(): lax.ppermute(rows, 'x', [(i, (i + k) % NX) for i in range(NX)])]
    unnamed x13 -> x10, local copies, waits for them, and re-layouts: 10.7 us -> 3.11 us
    ppermute x0 -> x3, waiting for transfers between devices: none -> 6.14 us  [local(): lax.ppermute(rows, 'x', [(i, (i + k) % NX) for i in range(NX)])]
    broadcast_in_dim x10 -> x0, local copies, waits for them, and re-layouts: 3.73 us -> none  [the longest x7 2.97 us: gather(): return swap(jnp.broadcast_to(value[None], (count,) + value.shape), axes)]
    slice x5 -> x0, local copies, waits for them, and re-layouts: 3.11 us -> none  [the longest x1 0.79 us: local(): cols = jnp.concatenate([piece[:HALF], bottom], axis=1)]
  transfers between devices with their start and end apart: 4 -> 4, of which waited for: 4 -> 2; matrix products, arithmetic and copies ran while one was open for 3% -> 0% of each run, Pallas kernels for 0% -> 0%
where the time goes in v2:
time: 121 us; the launch traced here: 120 us
  blocking collectives  79.1 us (65%)
  starting transfers between devices  25.1 us (21%)
  waiting for transfers between devices  6.15 us (5%)
  Pallas kernels  5.84 us (5%)
  local copies, waits for them, and re-layouts  3.11 us (3%)
    all_to_all x6, blocking collectives, swap(): return lax.all_to_all(value, axes, 0, 0, tiled=True)  76.6 us
    all_to_all x1, starting transfers between devices, swap(): return lax.all_to_all(value, axes, 0, 0, tiled=True)  15.7 us
    ppermute x3, starting transfers between devices, local(): lax.ppermute(rows, 'x', [(i, (i + k) % NX) for i in range(NX)])  9.32 us
    ppermute x3, waiting for transfers between devices, local(): lax.ppermute(rows, 'x', [(i, (i + k) % NX) for i in range(NX)])  6.14 us
    pallas_call x8, Pallas kernels, call(): pl.pallas_call(kernel, out_shape=outs, in_specs=[whole] * len(args), out_...  5.84 us
    unnamed x10, local copies, waits for them, and re-layouts  3.11 us
    all_gather x1, blocking collectives, local(): rows = lax.all_gather(rows, 'core')  2.5 us
  transfers between devices with their start and end apart: 4, of which 2 were waited for; matrix products, arithmetic and copies ran while one was open for 0% of the time, Pallas kernels for 0%

profile of v2, /device:TPU:1, one launch (start us, length us, event | category | flops | bytes accessed | tf_op | source)
XLA Modules:
  0.0 120.0 jit_solution(9543392497579149853)
XLA Ops:
  0.6 0.9 copy-done
  1.5 0.8 copy-done.1
  2.4 0.7 copy-done.2
  3.1 0.7 copy-done.3
  3.7 0.8 shard_map.59
  4.5 15.7 %all-to-all-start = ((f32[16,1,3328]{2,1,0:T(1,128)}), f32[16,1,3328]{2,1,0:T(1,128)S(1)}, u32[]{:S(2)}, u32[]{:S(2)}) async-start(f32[16,1,3328]{2,1,0:T(1,128)} %bitcast.3), calls=%async_computation | async-start | bytes 425984 | tf_op jit(solution)/shard_map/all_to_all | solution.py:199
  20.3 2.5 %all-gather = f32[128,256]{1,0:T(8,128)S(1)} all-gather(f32[64,256]{1,0:T(8,128)S(1)} %get-tuple-element.10), channel_id=2, replica_groups=mesh['y'=4,'x'=4,'core'=2,'z'=16] {'core'}, dimensions={0}, use_global_device_ids=true | all-gather | bytes 196608 | tf_op jit(solution)/shard_map/all_gather | solution.py:208
  22.8 4.4 %collective-permute-start.2 = (f32[2,64,256]{2,1,0:T(8,128)S(1)}, f32[2,64,256]{2,1,0:T(8,128)S(1)}, u32[]{:S(2)}, u32[]{:S(2)}) collective-permute-start(f32[2,64,256]{2,1,0:T(8,128)S(1)} %bitcast.8), channel_id=1, source_target_pairs={{0,96},{32,0},{64,32},{96,64},{1,97},{33,1},{65,33},{97,65},{2,98}... | collective-permute-start | bytes 393224 | tf_op jit(solution)/shard_map/ppermute | solution.py:209
  27.2 2.4 %collective-permute-start.1 = (f32[2,64,256]{2,1,0:T(8,128)S(1)}, f32[2,64,256]{2,1,0:T(8,128)S(1)}, u32[]{:S(2)}, u32[]{:S(2)}) collective-permute-start(f32[2,64,256]{2,1,0:T(8,128)S(1)} %bitcast.9), channel_id=1, source_target_pairs={{0,64},{32,96},{64,0},{96,32},{1,65},{33,97},{65,1},{97,33},{2,66}... | collective-permute-start | bytes 393224 | tf_op jit(solution)/shard_map/ppermute | solution.py:209
  29.6 2.5 %collective-permute-start = (f32[2,64,256]{2,1,0:T(8,128)S(1)}, f32[2,64,256]{2,1,0:T(8,128)S(1)}, u32[]{:S(2)}, u32[]{:S(2)}) collective-permute-start(f32[2,64,256]{2,1,0:T(8,128)S(1)} %bitcast.10), channel_id=1, source_target_pairs={{0,32},{32,64},{64,96},{96,0},{1,33},{33,65},{65,97},{97,1},{2,34}... | collective-permute-start | bytes 393224 | tf_op jit(solution)/shard_map/ppermute | solution.py:209
  32.1 2.8 %collective-permute-done.1.two_ref = f32[2,64,256]{2,1,0:T(8,128)S(1)} collective-permute-done((f32[2,64,256]{2,1,0:T(8,128)S(1)}, f32[2,64,256]{2,1,0:T(8,128)S(1)}, u32[]{:S(2)}, u32[]{:S(2)}) %collective-permute-start.1) | collective-permute-done | bytes 131104 | tf_op jit(solution)/shard_map/ppermute | solution.py:209
  35.0 3.3 %collective-permute-done.one_ref = f32[2,64,256]{2,1,0:T(8,128)S(1)} collective-permute-done((f32[2,64,256]{2,1,0:T(8,128)S(1)}, f32[2,64,256]{2,1,0:T(8,128)S(1)}, u32[]{:S(2)}, u32[]{:S(2)}) %collective-permute-start) | collective-permute-done | bytes 131104 | tf_op jit(solution)/shard_map/ppermute | solution.py:209
  38.3 1.7 %shard_map.60 = (f32[1024,2048]{1,0:T(8,128)S(1)}, f32[8,1,2048]{2,1,0:T(1,128)S(1)}, f32[1,2048]{1,0:T(1,128)S(1)}, f32[1,1024]{1,0:T(1,128)S(1)}) custom-call(f32[2,64,256]{2,1,0:T(8,128)S(1)} %bitcast.11, f32[2,64,256]{2,1,0:T(8,128)S(1)} %collective-permute-done.one_ref, f32[2,64,256]{2,1,0:T(8,128)S(1)} %collective-permute-done.1.two_ref, ...), custom_call_target="tpu_custom_call" | custom-call | tf_op jit(solution)/shard_map/pallas_call | solution.py:188
  39.9 8.8 %all_to_all.35.parts_ref = f32[8,1,2048]{2,1,0:T(1,128)S(1)} all-to-all(f32[8,1,2048]{2,1,0:T(1,128)S(1)} %get-tuple-element.13), channel_id=1, replica_groups=mesh['y'=4,'x'=4,'core'=2,'z'=16] {'x','core'}, dimensions={0} | all-to-all | bytes 131072 | tf_op jit(solution)/shard_map/all_to_all | solution.py:199
  48.8 0.7 shard_map.61
  49.4 8.2 %all_to_all.36.parts_ref = f32[4,1,1024]{2,1,0:T(1,128)S(1)} all-to-all(f32[4,1,1024]{2,1,0:T(1,128)S(1)} %shard_map.61), channel_id=1, replica_groups=mesh['y'=4,'x'=4,'core'=2,'z'=16] {'y'}, dimensions={0} | all-to-all | bytes 32768 | tf_op jit(solution)/shard_map/all_to_all | solution.py:199
  57.6 22.7 %all_to_all.37.parts_ref = f32[16,1,1024]{2,1,0:T(1,128)S(1)} all-to-all(f32[16,1,1024]{2,1,0:T(1,128)S(1)} %shard_map.62), channel_id=1, replica_groups=mesh['y'=4,'x'=4,'core'=2,'z'=16] {'z'}, dimensions={0} | all-to-all | bytes 131072 | tf_op jit(solution)/shard_map/all_to_all | solution.py:199
  80.4 0.7 shard_map.63
  81.1 10.9 %all_to_all.38.parts_ref = f32[8,1,2048]{2,1,0:T(1,128)S(1)} all-to-all(f32[8,1,2048]{2,1,0:T(1,128)S(1)} %shard_map.63), channel_id=1, replica_groups=mesh['y'=4,'x'=4,'core'=2,'z'=16] {'x','core'}, dimensions={0} | all-to-all | bytes 131072 | tf_op jit(solution)/shard_map/all_to_all | solution.py:199
  92.0 0.7 shard_map.64
  92.7 13.8 %all_to_all.39.landed_ref = f32[16,1,384]{2,1,0:T(1,128)S(1)} all-to-all(f32[16,1,384]{2,1,0:T(1,128)S(1)} %shard_map.64), channel_id=1, replica_groups=mesh['y'=4,'x'=4,'core'=2,'z'=16] {'z'}, dimensions={0} | all-to-all | bytes 49152 | tf_op jit(solution)/shard_map/all_to_all | solution.py:199
  106.6 0.6 shard_map.65
  107.2 12.1 %all_to_all.40.parts_ref = f32[32,1,128]{2,1,0:T(1,128)S(1)} all-to-all(f32[32,1,128]{2,1,0:T(1,128)S(1)} %get-tuple-element.17), channel_id=1, replica_groups=mesh['y'=4,'x'=4,'core'=2,'z'=16] {'y','x','core'}, dimensions={0} | all-to-all | bytes 32768 | tf_op jit(solution)/shard_map/all_to_all | solution.py:199
  119.3 0.7 shard_map.66
  (9 shorter events, 0.0 us)
Async XLA Ops:
  0.6 0.9 copy-start
  1.5 0.8 copy-start.1
  2.3 0.7 copy-start.2
  3.1 0.7 copy-start.3
  4.5 33.8 %all-to-all-start = ((f32[16,1,3328]{2,1,0:T(1,128)}), f32[16,1,3328]{2,1,0:T(1,128)S(1)}, u32[]{:S(2)}, u32[]{:S(2)}) async-start(f32[16,1,3328]{2,1,0:T(1,128)} %bitcast.3), calls=%async_computation | async-start | bytes 425984 | tf_op jit(solution)/shard_map/all_to_all | solution.py:199
  22.8 9.3 %collective-permute-start.2 = (f32[2,64,256]{2,1,0:T(8,128)S(1)}, f32[2,64,256]{2,1,0:T(8,128)S(1)}, u32[]{:S(2)}, u32[]{:S(2)}) collective-permute-start(f32[2,64,256]{2,1,0:T(8,128)S(1)} %bitcast.8), channel_id=1, source_target_pairs={{0,96},{32,0},{64,32},{96,64},{1,97},{33,1},{65,33},{97,65},{2,98}... | collective-permute-start | bytes 393224 | tf_op jit(solution)/shard_map/ppermute | solution.py:209
  27.2 7.8 %collective-permute-start.1 = (f32[2,64,256]{2,1,0:T(8,128)S(1)}, f32[2,64,256]{2,1,0:T(8,128)S(1)}, u32[]{:S(2)}, u32[]{:S(2)}) collective-permute-start(f32[2,64,256]{2,1,0:T(8,128)S(1)} %bitcast.9), channel_id=1, source_target_pairs={{0,64},{32,96},{64,0},{96,32},{1,65},{33,97},{65,1},{97,33},{2,66}... | collective-permute-start | bytes 393224 | tf_op jit(solution)/shard_map/ppermute | solution.py:209
  29.6 8.7 %collective-permute-start = (f32[2,64,256]{2,1,0:T(8,128)S(1)}, f32[2,64,256]{2,1,0:T(8,128)S(1)}, u32[]{:S(2)}, u32[]{:S(2)}) collective-permute-start(f32[2,64,256]{2,1,0:T(8,128)S(1)} %bitcast.10), channel_id=1, source_target_pairs={{0,32},{32,64},{64,96},{96,0},{1,33},{33,65},{65,97},{97,1},{2,34}... | collective-permute-start | bytes 393224 | tf_op jit(solution)/shard_map/ppermute | solution.py:209
  80.4 38.9 %copy-start.4 = (f32[512]{0:T(512)S(1)}, f32[512]{0:T(512)}, u32[]{:S(2)}) copy-start(f32[512]{0:T(512)} %param.7) | copy-start | bytes 6148

commit v3 on v2

--- a/solution.py
+++ b/solution.py
@@ -16,6 +16,7 @@
 PIECE = 64
 OWN = 256
 EPS = 2.0
+FULL = 60 << 20
 
 
 def split(value):
@@ -37,17 +38,32 @@
     return row, jnp.where(keep, cells, 0.0)
 
 
-def pack_kernel(src_ref, tgt_ref, src_mass_ref, tgt_mass_ref, rows_ref, cols_ref):
+def pack_kernel(tgt_ref, tgt_mass_ref, src_ref, src_mass_ref, cols_ref, rows_ref, tgt_buf, tgt_mass_buf, src_buf, src_mass_buf, sems):
     x, core, z = (lax.axis_index(name) for name in ("x", "core", "z"))
+    here = pl.ds(pl.multiple_of(x * 128, 128), 128)
+    copies = [
+        pltpu.make_async_copy(source, target, sems.at[k])
+        for k, (source, target) in enumerate(
+            (
+                (tgt_ref.at[:, here], tgt_buf),
+                (tgt_mass_ref, tgt_mass_buf),
+                (src_ref, src_buf),
+                (src_mass_ref, src_mass_buf),
+            )
+        )
+    ]
+    for copy in copies:
+        copy.start()
     rows_ref[...] = jnp.zeros_like(rows_ref)
-    rows_ref[0:HALF] = src_ref[0:HALF]
-    rows_ref[32 : 32 + PC - HALF] = src_ref[HALF:PC]
+    for copy in copies:
+        copy.wait()
+    rows_ref[0:HALF] = src_buf[0:HALF]
+    rows_ref[32 : 32 + PC - HALF] = src_buf[HALF:PC]
     for k in range(2):
-        rows_ref[MASS : MASS + 1, k * 128 : (k + 1) * 128] = src_mass_ref[pl.ds(2 * z + k, 1)]
-    here = pl.ds(pl.multiple_of(x * 128, 128), 128)
-    cells = tgt_ref[:, here]
+        rows_ref[MASS : MASS + 1, k * 128 : (k + 1) * 128] = src_mass_buf[pl.ds(2 * z + k, 1)]
+    cells = tgt_buf[...]
     top = cells[0:HALF]
-    bottom = jnp.concatenate([cells[HALF:PC], tgt_mass_ref[pl.ds(x, 1)], jnp.zeros((1, 128), jnp.float32)], axis=0)
+    bottom = jnp.concatenate([cells[HALF:PC], tgt_mass_buf[pl.ds(x, 1)], jnp.zeros((1, 128), jnp.float32)], axis=0)
     lane = lax.broadcasted_iota(jnp.int32, (HALF, 128), 1)
     first = jnp.where(lane < PIECE, top, pltpu.roll(bottom, PIECE, 1))
     second = jnp.where(lane < PIECE, pltpu.roll(top, PIECE, 1), bottom)
@@ -56,7 +72,7 @@
         cols_ref[k * HALF : (k + 1) * HALF] = piece
 
 
-def gibbs_kernel(own_ref, one_ref, two_ref, three_ref, cols_ref, gibbs_ref, part_ref, row_mass_ref, col_mass_ref, x_ref, y_ref):
+def stack_kernel(own_ref, one_ref, two_ref, three_ref, x_ref, row_mass_ref):
     x = lax.axis_index("x")
     for k, rows_ref in enumerate((own_ref, one_ref, two_ref, three_ref)):
         base = pl.multiple_of(lax.rem(x + NX - k, NX) * (NC * OWN), NC * OWN)
@@ -73,6 +89,9 @@
             x_ref[64:128, here] = high
             x_ref[128:192, here] = low
             x_ref[192:256, here] = low
+
+
+def gibbs_kernel(x_ref, cols_ref, gibbs_ref, part_ref, col_mass_ref, y_ref):
     lane = lax.broadcasted_iota(jnp.int32, (32, 128), 1)
     gap = jnp.zeros((32 - HALF, 128), jnp.float32)
     for t in range(NZ // 2):
@@ -162,16 +181,17 @@
             part_ref[k, :, i * 128 : (i + 1) * 128] = total
 
 
-def landing_kernel(landed_ref, rows_ref, part_ref):
-    total = jnp.zeros((1, 128), jnp.float32)
-    for k in range(NZ):
-        rows_ref[k] = EPS * jnp.log(landed_ref[k, :, 0:OWN])
+def landing_kernel(landed_ref, part_ref):
+    total = landed_ref[0, :, OWN : OWN + 128]
+    for k in range(1, NZ):
         total = total + landed_ref[k, :, OWN : OWN + 128]
     for k in range(NY * NG):
         part_ref[k] = total
 
 
-def potential_kernel(parts_ref, mass_ref, out_ref):
+def potential_kernel(landed_ref, parts_ref, mass_ref, rows_ref, out_ref):
+    for k in range(NZ):
+        rows_ref[k] = EPS * jnp.log(landed_ref[k, :, 0:OWN])
     lane = lax.broadcasted_iota(jnp.int32, (1, 128), 1)
     for t in range(NG // 2):
         a, b = (sum(parts_ref[y * NG + g] for y in range(NY)) for g in (2 * t, 2 * t + 1))
@@ -183,15 +203,15 @@
     return jax.ShapeDtypeStruct(shape, jnp.float32)
 
 
-def call(kernel, outs, *args, scratch=()):
+def call(kernel, outs, *args, scratch=(), space=pltpu.VMEM, limit=24 << 20):
     whole = pl.BlockSpec(memory_space=pltpu.VMEM)
     return pl.pallas_call(
         kernel,
         out_shape=outs,
-        in_specs=[whole] * len(args),
+        in_specs=[pl.BlockSpec(memory_space=space)] * len(args),
         out_specs=[whole] * len(outs),
         scratch_shapes=list(scratch),
-        compiler_params=pltpu.CompilerParams(vmem_limit_bytes=24 << 20),
+        compiler_params=pltpu.CompilerParams(vmem_limit_bytes=limit),
     )(*args)
 
 
@@ -201,19 +221,30 @@
 
 def local(src_cells, tgt_cells, src_mass, tgt_mass):
     tgt_mass = tgt_mass.reshape(NX, 128)
-    rows, cols = call(
-        pack_kernel, (f32(64, OWN), f32(NZ * HALF, 128)), src_cells, tgt_cells, src_mass.reshape(NZ * 2, 128), tgt_mass
+    cols, rows = call(
+        pack_kernel,
+        (f32(NZ * HALF, 128), f32(64, OWN)),
+        tgt_cells,
+        tgt_mass,
+        src_cells,
+        src_mass.reshape(NZ * 2, 128),
+        scratch=[pltpu.VMEM(shape, jnp.float32) for shape in ((PC, 128), (NX, 128), (PC, OWN), (NZ * 2, 128))]
+        + [pltpu.SemaphoreType.DMA((4,))],
+        space=pltpu.HBM,
+        limit=FULL,
     )
     cols = swap(cols.reshape(NZ, 1, HALF * 128), "z").reshape(NZ * HALF, 128)
     rows = lax.all_gather(rows, "core")
     others = [lax.ppermute(rows, "x", [(i, (i + k) % NX) for i in range(NX)]) for k in range(1, NX)]
-    gibbs, row_parts, row_mass, col_mass = call(
+    stack, row_mass = call(
+        stack_kernel, (jax.ShapeDtypeStruct((256, ROWS), jnp.bfloat16), f32(1, ROWS)), rows, *others
+    )
+    gibbs, row_parts, col_mass = call(
         gibbs_kernel,
-        (f32(COLS, ROWS), f32(NG, 1, ROWS), f32(1, ROWS), f32(1, COLS)),
-        rows,
-        *others,
+        (f32(COLS, ROWS), f32(NG, 1, ROWS), f32(1, COLS)),
+        stack,
         cols,
-        scratch=(pltpu.VMEM((256, ROWS), jnp.bfloat16), pltpu.VMEM((COLS, 256), jnp.bfloat16)),
+        scratch=(pltpu.VMEM((COLS, 256), jnp.bfloat16),),
     )
     scale = pltpu.VMEM((1, ROWS), jnp.float32)
     (col_parts,) = call(
@@ -225,8 +256,11 @@
     (leaving,) = call(
         last_column_kernel, (f32(NZ, 1, OWN + 128),), gibbs, swap(row_parts, GROUP), row_mass, scratch=(scale,)
     )
-    row_out, col_parts = call(landing_kernel, (f32(NZ, 1, OWN), f32(NY * NG, 1, 128)), swap(leaving, "z"))
-    (col_out,) = call(potential_kernel, (f32(NX, 128),), swap(col_parts, PLANE), tgt_mass)
+    landed = swap(leaving, "z")
+    (col_parts,) = call(landing_kernel, (f32(NY * NG, 1, 128),), landed)
+    row_out, col_out = call(
+        potential_kernel, (f32(NZ, 1, OWN), f32(NX, 128)), landed, swap(col_parts, PLANE), tgt_mass
+    )
     return row_out.reshape(NZ * OWN), col_out.reshape(NX * 128)
 
 

time: 121 us -> 118 us (0.975)
  local copies, waits for them, and re-layouts: 3.11 us -> 0.01 us
    unnamed x10 -> x2, local copies, waits for them, and re-layouts: 3.11 us -> 0.01 us
    pallas_call x8 -> x9, Pallas kernels: 5.84 us -> 6.14 us  [call(): pl.pallas_call(kernel, out_shape=outs, in_specs=[pl.BlockSpec(memory_spac...]
where the time goes in v3:
time: 118 us; the launch traced here: 117 us
  blocking collectives  79.3 us (67%)
  starting transfers between devices  25.1 us (21%)
  waiting for transfers between devices  6.15 us (5%)
  Pallas kernels  6.14 us (5%)
    all_to_all x6, blocking collectives, swap(): return lax.all_to_all(value, axes, 0, 0, tiled=True)  76.6 us
    all_to_all x1, starting transfers between devices, swap(): return lax.all_to_all(value, axes, 0, 0, tiled=True)  15.8 us
    ppermute x3, starting transfers between devices, local(): lax.ppermute(rows, 'x', [(i, (i + k) % NX) for i in range(NX)])  9.32 us
    ppermute x3, waiting for transfers between devices, local(): lax.ppermute(rows, 'x', [(i, (i + k) % NX) for i in range(NX)])  6.14 us
    pallas_call x9, Pallas kernels, call(): pl.pallas_call(kernel, out_shape=outs, in_specs=[pl.BlockSpec(memory_spac...  6.14 us
    all_gather x1, blocking collectives, local(): rows = lax.all_gather(rows, 'core')  2.72 us
  transfers between devices with their start and end apart: 4, of which 2 were waited for; matrix products, arithmetic and copies ran while one was open for 0% of the time, Pallas kernels for 0%

profile of v3, /device:TPU:1, one launch (start us, length us, event | category | flops | bytes accessed | tf_op | source)
XLA Modules:
  0.0 117.4 jit_solution(17105462613554648701)
XLA Ops:
  0.6 1.7 %shard_map.59 = (f32[416,128]{1,0:T(8,128)}, f32[64,256]{1,0:T(8,128)}) custom-call(f32[50,512]{1,0:T(8,128)} %tgt_ref.1, f32[4,128]{1,0:T(4,128)} %bitcast.12, f32[50,256]{1,0:T(8,128)} %src_ref.1, f32[32,128]{1,0:T(8,128)} %bitcast.15), custom_call_target="tpu_custom_call" | custom-call | tf_op jit(solution)/shard_map/pallas_call | solution.py:208
  2.3 15.8 %all-to-all-start = ((f32[16,1,3328]{2,1,0:T(1,128)}), f32[16,1,3328]{2,1,0:T(1,128)S(1)}, u32[]{:S(2)}, u32[]{:S(2)}) async-start(f32[16,1,3328]{2,1,0:T(1,128)} %bitcast.14), calls=%async_computation | async-start | bytes 425984 | tf_op jit(solution)/shard_map/all_to_all | solution.py:219
  18.1 2.7 %all-gather = f32[128,256]{1,0:T(8,128)S(1)} all-gather(f32[64,256]{1,0:T(8,128)} %get-tuple-element.11), channel_id=2, replica_groups=mesh['y'=4,'x'=4,'core'=2,'z'=16] {'core'}, dimensions={0}, use_global_device_ids=true | all-gather | bytes 196608 | tf_op jit(solution)/shard_map/all_gather | solution.py:237
  20.8 4.4 %collective-permute-start.2 = (f32[2,64,256]{2,1,0:T(8,128)S(1)}, f32[2,64,256]{2,1,0:T(8,128)S(1)}, u32[]{:S(2)}, u32[]{:S(2)}) collective-permute-start(f32[2,64,256]{2,1,0:T(8,128)S(1)} %bitcast.8), channel_id=1, source_target_pairs={{0,96},{32,0},{64,32},{96,64},{1,97},{33,1},{65,33},{97,65},{2,98}... | collective-permute-start | bytes 393224 | tf_op jit(solution)/shard_map/ppermute | solution.py:238
  25.2 2.4 %collective-permute-start.1 = (f32[2,64,256]{2,1,0:T(8,128)S(1)}, f32[2,64,256]{2,1,0:T(8,128)S(1)}, u32[]{:S(2)}, u32[]{:S(2)}) collective-permute-start(f32[2,64,256]{2,1,0:T(8,128)S(1)} %bitcast.9), channel_id=1, source_target_pairs={{0,64},{32,96},{64,0},{96,32},{1,65},{33,97},{65,1},{97,33},{2,66}... | collective-permute-start | bytes 393224 | tf_op jit(solution)/shard_map/ppermute | solution.py:238
  27.6 2.5 %collective-permute-start = (f32[2,64,256]{2,1,0:T(8,128)S(1)}, f32[2,64,256]{2,1,0:T(8,128)S(1)}, u32[]{:S(2)}, u32[]{:S(2)}) collective-permute-start(f32[2,64,256]{2,1,0:T(8,128)S(1)} %bitcast.10), channel_id=1, source_target_pairs={{0,32},{32,64},{64,96},{96,0},{1,33},{33,65},{65,97},{97,1},{2,34}... | collective-permute-start | bytes 393224 | tf_op jit(solution)/shard_map/ppermute | solution.py:238
  30.1 0.0 collective-permute-done.2.three_ref
  30.2 2.8 %collective-permute-done.1.two_ref = f32[2,64,256]{2,1,0:T(8,128)S(1)} collective-permute-done((f32[2,64,256]{2,1,0:T(8,128)S(1)}, f32[2,64,256]{2,1,0:T(8,128)S(1)}, u32[]{:S(2)}, u32[]{:S(2)}) %collective-permute-start.1) | collective-permute-done | bytes 131104 | tf_op jit(solution)/shard_map/ppermute | solution.py:238
  33.0 3.3 %collective-permute-done.one_ref = f32[2,64,256]{2,1,0:T(8,128)S(1)} collective-permute-done((f32[2,64,256]{2,1,0:T(8,128)S(1)}, f32[2,64,256]{2,1,0:T(8,128)S(1)}, u32[]{:S(2)}, u32[]{:S(2)}) %collective-permute-start) | collective-permute-done | bytes 131104 | tf_op jit(solution)/shard_map/ppermute | solution.py:238
  36.3 0.2 shard_map.60
  36.5 0.0 all-to-all-done
  36.5 1.5 %shard_map.61 = (f32[1024,2048]{1,0:T(8,128)S(1)}, f32[8,1,2048]{2,1,0:T(1,128)S(1)}, f32[1,1024]{1,0:T(1,128)S(1)}) custom-call(bf16[256,2048]{1,0:T(8,128)(2,1)S(1)} %get-tuple-element.12.x_ref, f32[416,128]{1,0:T(8,128)S(1)} %bitcast.7), custom_call_target="tpu_custom_call" | custom-call | tf_op jit(solution)/shard_map/pallas_call | solution.py:208
  38.0 8.4 %all_to_all.35.parts_ref = f32[8,1,2048]{2,1,0:T(1,128)S(1)} all-to-all(f32[8,1,2048]{2,1,0:T(1,128)S(1)} %get-tuple-element.15), channel_id=1, replica_groups=mesh['y'=4,'x'=4,'core'=2,'z'=16] {'x','core'}, dimensions={0} | all-to-all | bytes 131072 | tf_op jit(solution)/shard_map/all_to_all | solution.py:219
  46.5 0.6 shard_map.62
  47.1 8.2 %all_to_all.36.parts_ref = f32[4,1,1024]{2,1,0:T(1,128)S(1)} all-to-all(f32[4,1,1024]{2,1,0:T(1,128)S(1)} %shard_map.62), channel_id=1, replica_groups=mesh['y'=4,'x'=4,'core'=2,'z'=16] {'y'}, dimensions={0} | all-to-all | bytes 32768 | tf_op jit(solution)/shard_map/all_to_all | solution.py:219
  55.3 23.1 %all_to_all.37.parts_ref = f32[16,1,1024]{2,1,0:T(1,128)S(1)} all-to-all(f32[16,1,1024]{2,1,0:T(1,128)S(1)} %shard_map.63), channel_id=1, replica_groups=mesh['y'=4,'x'=4,'core'=2,'z'=16] {'z'}, dimensions={0} | all-to-all | bytes 131072 | tf_op jit(solution)/shard_map/all_to_all | solution.py:219
  78.4 0.0 copy-start
  78.4 0.7 shard_map.64
  79.1 10.9 %all_to_all.38.parts_ref = f32[8,1,2048]{2,1,0:T(1,128)S(1)} all-to-all(f32[8,1,2048]{2,1,0:T(1,128)S(1)} %shard_map.64), channel_id=1, replica_groups=mesh['y'=4,'x'=4,'core'=2,'z'=16] {'x','core'}, dimensions={0} | all-to-all | bytes 131072 | tf_op jit(solution)/shard_map/all_to_all | solution.py:219
  90.1 0.7 shard_map.65
  90.8 13.8 %all_to_all.39.landed_ref = f32[16,1,384]{2,1,0:T(1,128)S(1)} all-to-all(f32[16,1,384]{2,1,0:T(1,128)S(1)} %shard_map.65), channel_id=1, replica_groups=mesh['y'=4,'x'=4,'core'=2,'z'=16] {'z'}, dimensions={0} | all-to-all | bytes 49152 | tf_op jit(solution)/shard_map/all_to_all | solution.py:219
  104.6 12.1 %all_to_all.40.parts_ref = f32[32,1,128]{2,1,0:T(1,128)S(1)} all-to-all(f32[32,1,128]{2,1,0:T(1,128)S(1)} %shard_map.66), channel_id=1, replica_groups=mesh['y'=4,'x'=4,'core'=2,'z'=16] {'y','x','core'}, dimensions={0} | all-to-all | bytes 32768 | tf_op jit(solution)/shard_map/all_to_all | solution.py:219
  116.7 0.0 copy-done
  116.7 0.7 shard_map.67
  (2 shorter events, 0.0 us)
Async XLA Ops:
  2.3 34.2 %all-to-all-start = ((f32[16,1,3328]{2,1,0:T(1,128)}), f32[16,1,3328]{2,1,0:T(1,128)S(1)}, u32[]{:S(2)}, u32[]{:S(2)}) async-start(f32[16,1,3328]{2,1,0:T(1,128)} %bitcast.14), calls=%async_computation | async-start | bytes 425984 | tf_op jit(solution)/shard_map/all_to_all | solution.py:219
  20.8 9.3 %collective-permute-start.2 = (f32[2,64,256]{2,1,0:T(8,128)S(1)}, f32[2,64,256]{2,1,0:T(8,128)S(1)}, u32[]{:S(2)}, u32[]{:S(2)}) collective-permute-start(f32[2,64,256]{2,1,0:T(8,128)S(1)} %bitcast.8), channel_id=1, source_target_pairs={{0,96},{32,0},{64,32},{96,64},{1,97},{33,1},{65,33},{97,65},{2,98}... | collective-permute-start | bytes 393224 | tf_op jit(solution)/shard_map/ppermute | solution.py:238
  25.2 7.8 %collective-permute-start.1 = (f32[2,64,256]{2,1,0:T(8,128)S(1)}, f32[2,64,256]{2,1,0:T(8,128)S(1)}, u32[]{:S(2)}, u32[]{:S(2)}) collective-permute-start(f32[2,64,256]{2,1,0:T(8,128)S(1)} %bitcast.9), channel_id=1, source_target_pairs={{0,64},{32,96},{64,0},{96,32},{1,65},{33,97},{65,1},{97,33},{2,66}... | collective-permute-start | bytes 393224 | tf_op jit(solution)/shard_map/ppermute | solution.py:238
  27.6 8.7 %collective-permute-start = (f32[2,64,256]{2,1,0:T(8,128)S(1)}, f32[2,64,256]{2,1,0:T(8,128)S(1)}, u32[]{:S(2)}, u32[]{:S(2)}) collective-permute-start(f32[2,64,256]{2,1,0:T(8,128)S(1)} %bitcast.10), channel_id=1, source_target_pairs={{0,32},{32,64},{64,96},{96,0},{1,33},{33,65},{65,97},{97,1},{2,34}... | collective-permute-start | bytes 393224 | tf_op jit(solution)/shard_map/ppermute | solution.py:238
  78.4 38.3 %copy-start = (f32[512]{0:T(512)S(1)}, f32[512]{0:T(512)}, u32[]{:S(2)}) copy-start(f32[512]{0:T(512)} %param.7) | copy-start | bytes 6148

commit v4 on v3

v4 whole, which is shorter than its diff:
```python
import jax
import jax.numpy as jnp
from jax import lax
from jax.experimental import pallas as pl
from jax.experimental.pallas import tpu as pltpu
from jax.sharding import Mesh, PartitionSpec as P

NY, NH, NL, NC, NZ = 4, 2, 2, 2, 16
NX = NH * NL
NG = NL * NC
NS = NY * NH
PLANE = ("y", "half", "x", "core")
GROUP = ("x", "core")
PC = 50
STEP = 13
MASS = 59
QUARTER = 32
OWN = 256
ROWS, COLS = NG * OWN, NZ * 128
EPS = 2.0


def split(value):
    high = value.astype(jnp.bfloat16)
    low = (value - high.astype(jnp.float32)).astype(jnp.bfloat16)
    return high, low


def augmented(cells, norm_row, ones_row):
    row = lax.broadcasted_iota(jnp.int32, cells.shape, 0)
    keep = (lax.rem(row, 16) < STEP) & (row < MASS)
    cells = jnp.where(keep, cells, 0.0)
    norm = -0.5 * jnp.sum(cells * cells, axis=0, keepdims=True)
    first = norm.astype(jnp.bfloat16).astype(jnp.float32)
    rest = norm - first
    second = rest.astype(jnp.bfloat16).astype(jnp.float32)
    extra = jnp.where((row >= ones_row) & (row < ones_row + 3), 1.0, 0.0)
    for k, piece in enumerate((first, second, rest - second)):
        extra = jnp.where(row == norm_row + k, piece, extra)
    high, low = split(cells)
    return high, low, high.astype(jnp.float32) + extra


def pack_kernel(tgt_ref, tgt_mass_ref, src_ref, src_mass_ref, cols_ref, rows_ref, tgt_buf, tgt_mass_buf, src_buf, src_mass_buf, sems):
    y, x, core, z = (lax.axis_index(name) for name in ("y", "x", "core", "z"))
    me = x * NC + core
    here = pl.ds(pl.multiple_of(me * 128, 128), 128)
    pairs = (
        (tgt_ref.at[:, here], tgt_buf),
        (tgt_mass_ref, tgt_mass_buf),
        (src_ref, src_buf),
        (src_mass_ref, src_mass_buf),
    )
    copies = [pltpu.make_async_copy(a, b, sems.at[k]) for k, (a, b) in enumerate(pairs)]
    for copy in copies:
        copy.start()
    rows_ref[...] = jnp.zeros_like(rows_ref)
    for copy in copies:
        copy.wait()
    for q in range(4):
        rows_ref[16 * q : 16 * q + min(STEP, PC - STEP * q)] = src_buf[STEP * q : min(STEP * (q + 1), PC)]
    for k in range(2):
        rows_ref[MASS : MASS + 1, k * 128 : (k + 1) * 128] = src_mass_buf[pl.ds(2 * z + k, 1)]
    cells = jnp.concatenate([tgt_buf[...], tgt_mass_buf[pl.ds(me, 1)], jnp.zeros((5, 128), jnp.float32)], axis=0)
    cells = pltpu.roll(cells, lax.rem(128 - QUARTER * y, 128), 1)
    lane = lax.broadcasted_iota(jnp.int32, (STEP, 128), 1)
    piece = cells[0:STEP]
    for q in range(1, 4):
        moved = pltpu.roll(cells[STEP * q : STEP * (q + 1)], QUARTER * q, 1)
        piece = jnp.where(lane < QUARTER * q, piece, moved)
    for k in range(NZ):
        cols_ref[k * STEP : (k + 1) * STEP] = piece


def stack_kernel(rows_ref, x_ref, row_mass_ref):
    for g in range(NG):
        here = slice(g * OWN, (g + 1) * OWN)
        cells = rows_ref[g]
        row_mass_ref[:, here] = cells[MASS : MASS + 1]
        high, low, plus = augmented(cells, 13, 29)
        x_ref[0:64, here] = plus.astype(jnp.bfloat16)
        x_ref[64:128, here] = high
        x_ref[128:192, here] = low
        x_ref[192:256, here] = low


def copy_kernel(cols_ref, out_ref):
    value = cols_ref[...]
    for k in range(NY):
        out_ref[k] = value


def gibbs_kernel(x_ref, cols_ref, gibbs_ref, part_ref, col_mass_ref, y_ref):
    lane = lax.broadcasted_iota(jnp.int32, (16, 128), 1)
    gap = jnp.zeros((16 - STEP, 128), jnp.float32)
    for z in range(NZ):
        here = slice(z * 128, (z + 1) * 128)
        taken = [jnp.concatenate([cols_ref[y, z * STEP : (z + 1) * STEP], gap], axis=0) for y in range(NY)]
        groups = []
        for q in range(4):
            moved = [pltpu.roll(taken[y], QUARTER * (y - q) % 128, 1) if y != q else taken[y] for y in range(NY)]
            group = moved[0]
            for y in range(1, NY):
                group = jnp.where(lane < QUARTER * y, group, moved[y])
            groups.append(group)
        cells = jnp.concatenate(groups, axis=0)
        col_mass_ref[:, here] = cells[MASS : MASS + 1]
        high, low, plus = augmented(cells, 29, 13)
        turned = jnp.concatenate([plus, low.astype(jnp.float32)], axis=0).T.astype(jnp.bfloat16)
        y_ref[here, 0:128] = turned
        y_ref[here, 128:256] = turned
    for n in range(ROWS // 256):
        there = slice(n * 256, (n + 1) * 256)
        total = jnp.zeros((8, 256), jnp.float32)
        for m in range(COLS // 256):
            here = slice(m * 256, (m + 1) * 256)
            tile = jnp.exp(jnp.dot(y_ref[here, :], x_ref[:, there], preferred_element_type=jnp.float32))
            gibbs_ref[here, there] = tile
            total = total + jnp.sum(tile.reshape(32, 8, 256), axis=0)
        part_ref[:, there] = jnp.sum(total, axis=0, keepdims=True)


def summed(parts_ref):
    total = parts_ref[0]
    for k in range(1, parts_ref.shape[0]):
        total = total + parts_ref[k]
    return total


def columns(gibbs_ref, scale_ref, j):
    here = slice(j * 128, (j + 1) * 128)
    total = jnp.zeros((128, 128), jnp.float32)
    for i in range(ROWS // 128):
        there = slice(i * 128, (i + 1) * 128)
        total = total + gibbs_ref[here, there] * scale_ref[:, there]
    return jnp.sum(total.T, axis=0, keepdims=True)


def column_kernel(gibbs_ref, parts_ref, mass_ref, part_ref, scale_ref):
    scale_ref[...] = mass_ref[...] / summed(parts_ref)
    for j in range(COLS // 128):
        total = columns(gibbs_ref, scale_ref, j)
        for k in range(NS):
            part_ref[k, :, j * 128 : (j + 1) * 128] = total


def relay_kernel(parts_ref, part_ref):
    total = summed(parts_ref)
    for k in range(part_ref.shape[0]):
        part_ref[k] = total


def last_column_kernel(gibbs_ref, parts_ref, mass_ref, leaving_ref, scale_ref):
    scale_ref[...] = mass_ref[...] / summed(parts_ref)
    me = lax.axis_index("x") * NC + lax.axis_index("core")
    own = scale_ref[:, pl.ds(pl.multiple_of(me * OWN, OWN), OWN)]
    for j in range(NZ):
        leaving_ref[j, :, 0:OWN] = own
        leaving_ref[j, :, OWN : OWN + 128] = columns(gibbs_ref, scale_ref, j)


def row_kernel(gibbs_ref, parts_ref, mass_ref, part_ref):
    scale = mass_ref[...] / summed(parts_ref)
    totals = [jnp.zeros((8, 128), jnp.float32)] * (ROWS // 128)
    for j in range(COLS // 128):
        here = slice(j * 128, (j + 1) * 128)
        spread = jnp.broadcast_to(scale[:, here], (128, 128)).T
        for i in range(ROWS // 128):
            there = slice(i * 128, (i + 1) * 128)
            totals[i] = totals[i] + jnp.sum((gibbs_ref[here, there] * spread).reshape(16, 8, 128), axis=0)
    for i in range(ROWS // 128):
        part_ref[:, i * 128 : (i + 1) * 128] = jnp.sum(totals[i], axis=0, keepdims=True)


def landing_kernel(landed_ref, part_ref):
    total = landed_ref[0, :, OWN : OWN + 128]
    for k in range(1, NZ):
        total = total + landed_ref[k, :, OWN : OWN + 128]
    for k in range(NS * NG):
        part_ref[k] = total


def potential_kernel(landed_ref, parts_ref, mass_ref, rows_ref, out_ref):
    for k in range(NZ):
        rows_ref[k] = EPS * jnp.log(landed_ref[k, :, 0:OWN])
    for t in range(NG):
        total = parts_ref[t]
        for k in range(1, NS):
            total = total + parts_ref[k * NG + t]
        out_ref[t : t + 1] = EPS * jnp.log(mass_ref[t : t + 1] / total)


def f32(*shape):
    return jax.ShapeDtypeStruct(shape, jnp.float32)


def call(kernel, outs, *args, scratch=(), space=pltpu.VMEM, limit=24 << 20):
    whole = pl.BlockSpec(memory_space=pltpu.VMEM)
    return pl.pallas_call(
        kernel,
        out_shape=outs,
        in_specs=[pl.BlockSpec(memory_space=space)] * len(args),
        out_specs=[whole] * len(outs),
        scratch_shapes=list(scratch),
        compiler_params=pltpu.CompilerParams(vmem_limit_bytes=limit),
    )(*args)


def swap(value, axes):
    return lax.all_to_all(value, axes, 0, 0, tiled=True)


def local(src_cells, tgt_cells, src_mass, tgt_mass):
    tgt_mass = tgt_mass.reshape(NG, 128)
    cols, rows = call(
        pack_kernel,
        (f32(NZ * STEP, 128), f32(64, OWN)),
        tgt_cells,
        tgt_mass,
        src_cells,
        src_mass.reshape(NZ * 2, 128),
        scratch=[pltpu.VMEM(shape, jnp.float32) for shape in ((PC, 128), (NG, 128), (PC, OWN), (NZ * 2, 128))]
        + [pltpu.SemaphoreType.DMA((4,))],
        space=pltpu.HBM,
        limit=60 << 20,
    )
    cols = swap(cols.reshape(NZ, 1, STEP * 128), "z").reshape(NZ * STEP, 128)
    stack, row_mass = call(
        stack_kernel,
        (jax.ShapeDtypeStruct((256, ROWS), jnp.bfloat16), f32(1, ROWS)),
        lax.all_gather(rows, GROUP),
    )
    cols, stack = lax.optimization_barrier((cols, stack))
    (cols,) = call(copy_kernel, (f32(NY, NZ * STEP, 128),), cols)
    cols = swap(cols.reshape(NY, 1, NZ * STEP * 128), "y").reshape(NY, NZ * STEP, 128)
    gibbs, row_part, col_mass = call(
        gibbs_kernel,
        (f32(COLS, ROWS), f32(1, ROWS), f32(1, COLS)),
        stack,
        cols,
        scratch=(pltpu.VMEM((COLS, 256), jnp.bfloat16),),
    )
    scale = pltpu.VMEM((1, ROWS), jnp.float32)
    row_parts = lax.all_gather(row_part, GROUP)
    (col_parts,) = call(column_kernel, (f32(NS, 1, COLS),), gibbs, row_parts, row_mass, scratch=(scale,))
    (col_parts,) = call(relay_kernel, (f32(NZ, 1, COLS),), swap(col_parts, ("y", "half")))
    (row_part,) = call(row_kernel, (f32(1, ROWS),), gibbs, swap(col_parts, "z"), col_mass)
    row_parts = lax.all_gather(row_part, GROUP)
    (leaving,) = call(
        last_column_kernel, (f32(NZ, 1, OWN + 128),), gibbs, row_parts, row_mass, scratch=(scale,)
    )
    landed = swap(leaving, "z")
    (col_parts,) = call(landing_kernel, (f32(NS * NG, 1, 128),), landed)
    row_out, col_out = call(
        potential_kernel, (f32(NZ, 1, OWN), f32(NG, 128)), landed, swap(col_parts, PLANE), tgt_mass
    )
    return row_out.reshape(NZ * OWN), col_out.reshape(NG * 128)


def solution(mesh):
    grid = Mesh(mesh.devices.reshape(NY, NH, NL, NC, NZ), PLANE + ("z",))
    placed = (P(None, PLANE + ("z",)), P(None, "z"), P(PLANE), P("z"))
    return jax.shard_map(local, mesh=grid, in_specs=placed, out_specs=(P(PLANE), P("z")), check_vma=False)
```

time: 118 us -> 118 us (level)
  blocking collectives: 79.3 us -> 89.7 us
  starting transfers between devices: 25.1 us -> 15.8 us
    all_gather x1 -> x3, blocking collectives: 2.72 us -> 25 us  [the longest x2 18.2 us: local(): row_parts = lax.all_gather(row_part, GROUP)]
    all_to_all x6 -> x5, blocking collectives: 76.6 us -> 64.7 us  [swap(): return lax.all_to_all(value, axes, 0, 0, tiled=True)]
    ppermute x3 -> x0, starting transfers between devices: 9.32 us -> none  [local(): lax.ppermute(rows, 'x', [(i, (i + k) % NX) for i in range(NX)])]
    ppermute x3 -> x0, waiting for transfers between devices: 6.14 us -> none  [local(): lax.ppermute(rows, 'x', [(i, (i + k) % NX) for i in range(NX)])]
    all_to_all x1, waiting for transfers between devices: 0.01 us -> 4.98 us  [swap(): return lax.all_to_all(value, axes, 0, 0, tiled=True)]
    pallas_call x9 -> x10, Pallas kernels: 6.14 us -> 6.44 us  [call(): pl.pallas_call(kernel, out_shape=outs, in_specs=[pl.BlockSpec(memory_spac...]
  transfers between devices with their start and end apart: 4 -> 1, of which waited for: 2 -> 1; matrix products, arithmetic and copies ran while one was open for 0% -> 0% of each run, Pallas kernels for 0% -> 0%
where the time goes in v4:
time: 118 us
  blocking collectives  89.7 us (76%)
  starting transfers between devices  15.8 us (13%)
  Pallas kernels  6.44 us (5%)
  waiting for transfers between devices  4.98 us (4%)
    all_to_all x5, blocking collectives, swap(): return lax.all_to_all(value, axes, 0, 0, tiled=True)  64.7 us
    all_gather x2, blocking collectives, local(): row_parts = lax.all_gather(row_part, GROUP)  18.2 us
    all_to_all x1, starting transfers between devices, swap(): return lax.all_to_all(value, axes, 0, 0, tiled=True)  15.8 us
    all_gather x1, blocking collectives, local(): lax.all_gather(rows, GROUP)  6.79 us
    pallas_call x10, Pallas kernels, call(): pl.pallas_call(kernel, out_shape=outs, in_specs=[pl.BlockSpec(memory_spac...  6.44 us
    all_to_all x1, waiting for transfers between devices, swap(): return lax.all_to_all(value, axes, 0, 0, tiled=True)  4.98 us
  transfers between devices with their start and end apart: 1, of which 1 were waited for; matrix products, arithmetic and copies ran while one was open for 0% of the time, Pallas kernels for 0%

profile of v4, /device:TPU:1, one launch (start us, length us, event | category | flops | bytes accessed | tf_op | source)
XLA Modules:
  0.0 117.5 jit_solution(11617919278947982723)
XLA Ops:
  0.6 1.7 %shard_map.59 = (f32[208,128]{1,0:T(8,128)}, f32[64,256]{1,0:T(8,128)}) custom-call(f32[50,512]{1,0:T(8,128)} %tgt_ref.1, f32[4,128]{1,0:T(4,128)} %bitcast.16, f32[50,256]{1,0:T(8,128)} %src_ref.1, f32[32,128]{1,0:T(8,128)} %bitcast.20), custom_call_target="tpu_custom_call" | custom-call | tf_op jit(solution)/shard_map/pallas_call | solution.py:199
  2.4 15.8 %all-to-all-start = ((f32[16,1,1664]{2,1,0:T(1,128)}), f32[16,1,1664]{2,1,0:T(1,128)S(1)}, u32[]{:S(2)}, u32[]{:S(2)}) async-start(f32[16,1,1664]{2,1,0:T(1,128)} %bitcast.19), calls=%async_computation | async-start | bytes 212992 | tf_op jit(solution)/shard_map/all_to_all | solution.py:210
  18.1 6.8 %all-gather = f32[256,256]{1,0:T(8,128)S(1)} all-gather(f32[64,256]{1,0:T(8,128)} %get-tuple-element.14), channel_id=2, replica_groups=mesh['y'=4,'half'=2,'x'=2,'core'=2,'z'=16] {'x','core'}, dimensions={0}, use_global_device_ids=true | all-gather | bytes 327680 | tf_op jit(solution)/shard_map/all_gather | solution.py:231
  24.9 0.1 shard_map.60
  25.0 5.0 %all-to-all-done = f32[16,1,1664]{2,1,0:T(1,128)S(1)} async-done(((f32[16,1,1664]{2,1,0:T(1,128)}), f32[16,1,1664]{2,1,0:T(1,128)S(1)}, u32[]{:S(2)}, u32[]{:S(2)}) %all-to-all-start) | async-done | bytes 106528 | tf_op jit(solution)/shard_map/all_to_all | solution.py:210
  30.0 10.4 %all_to_all.30 = f32[4,1,26624]{2,1,0:T(1,128)S(1)} all-to-all(f32[4,1,26624]{2,1,0:T(1,128)S(1)} %bitcast.12), channel_id=1, replica_groups=mesh['y'=4,'half'=2,'x'=2,'core'=2,'z'=16] {'y'}, dimensions={0} | all-to-all | bytes 851968 | tf_op jit(solution)/shard_map/all_to_all | solution.py:210
  40.4 2.0 %shard_map.62 = (f32[2048,1024]{1,0:T(8,128)S(1)}, f32[1,1024]{1,0:T(1,128)S(1)}, f32[1,2048]{1,0:T(1,128)S(1)}) custom-call(bf16[256,1024]{1,0:T(8,128)(2,1)S(1)} %get-tuple-element.16.x_ref, f32[4,208,128]{2,1,0:T(8,128)S(1)} %bitcast.11), custom_call_target="tpu_custom_call" | custom-call | tf_op jit(solution)/shard_map/pallas_call | solution.py:199
  42.4 9.4 %all-gather.3.parts_ref = f32[4,1,1024]{2,1,0:T(1,128)S(1)} all-gather(f32[1,1,1024]{2,1,0:T(1,128)S(1)} %bitcast.18), channel_id=3, replica_groups=mesh['y'=4,'half'=2,'x'=2,'core'=2,'z'=16] {'x','core'}, dimensions={0}, use_global_device_ids=true | all-gather | bytes 20480 | tf_op jit(solution)/shard_map/all_gather | solution.py:244
  51.7 0.7 shard_map.63
  52.4 11.1 %all_to_all.31.parts_ref = f32[8,1,2048]{2,1,0:T(1,128)S(1)} all-to-all(f32[8,1,2048]{2,1,0:T(1,128)S(1)} %shard_map.63), channel_id=1, replica_groups=mesh['y'=4,'half'=2,'x'=2,'core'=2,'z'=16] {'y','half'}, dimensions={0} | all-to-all | bytes 131072 | tf_op jit(solution)/shard_map/all_to_all | solution.py:210
  63.5 17.2 %all_to_all.32.parts_ref = f32[16,1,2048]{2,1,0:T(1,128)S(1)} all-to-all(f32[16,1,2048]{2,1,0:T(1,128)S(1)} %shard_map.64), channel_id=1, replica_groups=mesh['y'=4,'half'=2,'x'=2,'core'=2,'z'=16] {'z'}, dimensions={0} | all-to-all | bytes 262144 | tf_op jit(solution)/shard_map/all_to_all | solution.py:210
  80.8 0.0 copy-start
  80.8 0.7 shard_map.65
  81.4 8.8 %all-gather.4.parts_ref = f32[4,1,1024]{2,1,0:T(1,128)S(1)} all-gather(f32[1,1,1024]{2,1,0:T(1,128)S(1)} %bitcast.15), channel_id=4, replica_groups=mesh['y'=4,'half'=2,'x'=2,'core'=2,'z'=16] {'x','core'}, dimensions={0}, use_global_device_ids=true | all-gather | bytes 20480 | tf_op jit(solution)/shard_map/all_gather | solution.py:248
  90.3 0.6 shard_map.66
  90.9 14.5 %all_to_all.33.landed_ref = f32[16,1,384]{2,1,0:T(1,128)S(1)} all-to-all(f32[16,1,384]{2,1,0:T(1,128)S(1)} %shard_map.66), channel_id=1, replica_groups=mesh['y'=4,'half'=2,'x'=2,'core'=2,'z'=16] {'z'}, dimensions={0} | all-to-all | bytes 49152 | tf_op jit(solution)/shard_map/all_to_all | solution.py:210
  105.5 11.4 %all_to_all.34.parts_ref = f32[32,1,128]{2,1,0:T(1,128)S(1)} all-to-all(f32[32,1,128]{2,1,0:T(1,128)S(1)} %shard_map.67), channel_id=1, replica_groups=mesh['y'=4,'half'=2,'x'=2,'core'=2,'z'=16] {'y','half','x','core'}, dimensions={0} | all-to-all | bytes 32768 | tf_op jit(solution)/shard_map/all_to_all | solution.py:210
  116.9 0.0 copy-done
  116.9 0.6 shard_map.68
  (3 shorter events, 0.1 us)
Async XLA Ops:
  2.4 27.6 %all-to-all-start = ((f32[16,1,1664]{2,1,0:T(1,128)}), f32[16,1,1664]{2,1,0:T(1,128)S(1)}, u32[]{:S(2)}, u32[]{:S(2)}) async-start(f32[16,1,1664]{2,1,0:T(1,128)} %bitcast.19), calls=%async_computation | async-start | bytes 212992 | tf_op jit(solution)/shard_map/all_to_all | solution.py:210
  80.8 36.1 %copy-start = (f32[512]{0:T(512)S(1)}, f32[512]{0:T(512)}, u32[]{:S(2)}) copy-start(f32[512]{0:T(512)} %param.7) | copy-start | bytes 6148

commit v5 on v3

--- a/solution.py
+++ b/solution.py
@@ -38,32 +38,20 @@
     return row, jnp.where(keep, cells, 0.0)
 
 
-def pack_kernel(tgt_ref, tgt_mass_ref, src_ref, src_mass_ref, cols_ref, rows_ref, tgt_buf, tgt_mass_buf, src_buf, src_mass_buf, sems):
-    x, core, z = (lax.axis_index(name) for name in ("x", "core", "z"))
+def pack_kernel(tgt_ref, tgt_mass_ref, cols_ref, cells_ref, mass_ref, sems):
+    x, core = lax.axis_index("x"), lax.axis_index("core")
     here = pl.ds(pl.multiple_of(x * 128, 128), 128)
-    copies = [
-        pltpu.make_async_copy(source, target, sems.at[k])
-        for k, (source, target) in enumerate(
-            (
-                (tgt_ref.at[:, here], tgt_buf),
-                (tgt_mass_ref, tgt_mass_buf),
-                (src_ref, src_buf),
-                (src_mass_ref, src_mass_buf),
-            )
-        )
-    ]
+    copies = (
+        pltpu.make_async_copy(tgt_ref.at[:, here], cells_ref, sems.at[0]),
+        pltpu.make_async_copy(tgt_mass_ref, mass_ref, sems.at[1]),
+    )
     for copy in copies:
         copy.start()
-    rows_ref[...] = jnp.zeros_like(rows_ref)
     for copy in copies:
         copy.wait()
-    rows_ref[0:HALF] = src_buf[0:HALF]
-    rows_ref[32 : 32 + PC - HALF] = src_buf[HALF:PC]
-    for k in range(2):
-        rows_ref[MASS : MASS + 1, k * 128 : (k + 1) * 128] = src_mass_buf[pl.ds(2 * z + k, 1)]
-    cells = tgt_buf[...]
+    cells = cells_ref[...]
     top = cells[0:HALF]
-    bottom = jnp.concatenate([cells[HALF:PC], tgt_mass_buf[pl.ds(x, 1)], jnp.zeros((1, 128), jnp.float32)], axis=0)
+    bottom = jnp.concatenate([cells[HALF:PC], mass_ref[pl.ds(x, 1)], jnp.zeros((1, 128), jnp.float32)], axis=0)
     lane = lax.broadcasted_iota(jnp.int32, (HALF, 128), 1)
     first = jnp.where(lane < PIECE, top, pltpu.roll(bottom, PIECE, 1))
     second = jnp.where(lane < PIECE, pltpu.roll(top, PIECE, 1), bottom)
@@ -72,26 +60,31 @@
         cols_ref[k * HALF : (k + 1) * HALF] = piece
 
 
-def stack_kernel(own_ref, one_ref, two_ref, three_ref, x_ref, row_mass_ref):
-    x = lax.axis_index("x")
-    for k, rows_ref in enumerate((own_ref, one_ref, two_ref, three_ref)):
-        base = pl.multiple_of(lax.rem(x + NX - k, NX) * (NC * OWN), NC * OWN)
-        for c in range(NC):
-            here = pl.ds(pl.multiple_of(base + c * OWN, OWN), OWN)
-            cells = rows_ref[c]
-            row_mass_ref[:, here] = cells[MASS : MASS + 1]
-            row, cells = masked(cells)
-            first, second, third = pieces(-0.5 * jnp.sum(cells * cells, axis=0, keepdims=True))
-            high, low = split(cells)
-            extra = jnp.where(row == 26, first, jnp.where(row == 27, second, jnp.where(row == 28, third, 0.0)))
-            extra = jnp.where((row >= 29) & (row < 32), 1.0, extra)
-            x_ref[0:64, here] = (high.astype(jnp.float32) + extra).astype(jnp.bfloat16)
-            x_ref[64:128, here] = high
-            x_ref[128:192, here] = low
-            x_ref[192:256, here] = low
-
-
-def gibbs_kernel(x_ref, cols_ref, gibbs_ref, part_ref, col_mass_ref, y_ref):
+def stack_kernel(rows_ref, mass_ref, x_ref, own_mass_ref):
+    z = lax.axis_index("z")
+    for k in range(2):
+        own_mass_ref[:, k * 128 : (k + 1) * 128] = mass_ref[pl.ds(2 * z + k, 1)]
+    for g in range(NG):
+        here = slice(g * OWN, (g + 1) * OWN)
+        cells = rows_ref[g]
+        norm = -0.5 * jnp.sum(cells * cells, axis=0, keepdims=True)
+        ones = jnp.ones((3, OWN), jnp.float32)
+        high, low = split(cells)
+        high = high.astype(jnp.float32)
+        low = low.astype(jnp.float32)
+        gap = jnp.zeros((8, OWN), jnp.float32)
+        plus = jnp.concatenate([high[0:HALF], *pieces(norm), ones, high[HALF:PC], gap], axis=0)
+        low = jnp.concatenate([low[0:HALF], gap[0:6], low[HALF:PC], gap], axis=0).astype(jnp.bfloat16)
+        row = lax.broadcasted_iota(jnp.int32, (64, OWN), 0)
+        x_ref[0:64, here] = plus.astype(jnp.bfloat16)
+        x_ref[64:128, here] = jnp.where((row < HALF) | (row >= 32), plus, 0.0).astype(jnp.bfloat16)
+        x_ref[128:192, here] = low
+        x_ref[192:256, here] = low
+
+
+def gibbs_kernel(x_ref, cols_ref, mass_ref, gibbs_ref, part_ref, col_mass_ref, y_ref):
+    for k in range(NG):
+        part_ref[k, :, ROWS : ROWS + OWN] = mass_ref[...]
     lane = lax.broadcasted_iota(jnp.int32, (32, 128), 1)
     gap = jnp.zeros((32 - HALF, 128), jnp.float32)
     for t in range(NZ // 2):
@@ -140,8 +133,13 @@
     return jnp.sum(total.T, axis=0, keepdims=True)
 
 
-def column_kernel(gibbs_ref, parts_ref, mass_ref, part_ref, scale_ref):
-    scale_ref[...] = mass_ref[...] / summed(parts_ref)
+def column_kernel(gibbs_ref, parts_ref, part_ref, mass_ref, scale_ref):
+    for k in range(NG):
+        mass_ref[:, k * OWN : (k + 1) * OWN] = parts_ref[k, :, ROWS : ROWS + OWN]
+    total = parts_ref[0, :, 0:ROWS]
+    for k in range(1, NG):
+        total = total + parts_ref[k, :, 0:ROWS]
+    scale_ref[...] = mass_ref[...] / total
     for j in range(COLS // 128):
         total = columns(gibbs_ref, scale_ref, j)
         for k in range(NY):
@@ -221,34 +219,33 @@
 
 def local(src_cells, tgt_cells, src_mass, tgt_mass):
     tgt_mass = tgt_mass.reshape(NX, 128)
-    cols, rows = call(
+    (cols,) = call(
         pack_kernel,
-        (f32(NZ * HALF, 128), f32(64, OWN)),
+        (f32(NZ * HALF, 128),),
         tgt_cells,
         tgt_mass,
-        src_cells,
+        scratch=[pltpu.VMEM((PC, 128), jnp.float32), pltpu.VMEM((NX, 128), jnp.float32), pltpu.SemaphoreType.DMA((2,))],
+        space=pltpu.HBM,
+        limit=60 << 20,
+    )
+    cols = swap(cols.reshape(NZ, 1, HALF * 128), "z").reshape(NZ * HALF, 128)
+    stack, own_mass = call(
+        stack_kernel,
+        (jax.ShapeDtypeStruct((256, ROWS), jnp.bfloat16), f32(1, OWN)),
+        lax.all_gather(src_cells, GROUP),
         src_mass.reshape(NZ * 2, 128),
-        scratch=[pltpu.VMEM(shape, jnp.float32) for shape in ((PC, 128), (NX, 128), (PC, OWN), (NZ * 2, 128))]
-        + [pltpu.SemaphoreType.DMA((4,))],
-        space=pltpu.HBM,
-        limit=FULL,
-    )
-    cols = swap(cols.reshape(NZ, 1, HALF * 128), "z").reshape(NZ * HALF, 128)
-    rows = lax.all_gather(rows, "core")
-    others = [lax.ppermute(rows, "x", [(i, (i + k) % NX) for i in range(NX)]) for k in range(1, NX)]
-    stack, row_mass = call(
-        stack_kernel, (jax.ShapeDtypeStruct((256, ROWS), jnp.bfloat16), f32(1, ROWS)), rows, *others
     )
     gibbs, row_parts, col_mass = call(
         gibbs_kernel,
-        (f32(COLS, ROWS), f32(NG, 1, ROWS), f32(1, COLS)),
+        (f32(COLS, ROWS), f32(NG, 1, ROWS + OWN), f32(1, COLS)),
         stack,
         cols,
+        own_mass,
         scratch=(pltpu.VMEM((COLS, 256), jnp.bfloat16),),
     )
     scale = pltpu.VMEM((1, ROWS), jnp.float32)
-    (col_parts,) = call(
-        column_kernel, (f32(NY, 1, COLS),), gibbs, swap(row_parts, GROUP), row_mass, scratch=(scale,)
+    col_parts, row_mass = call(
+        column_kernel, (f32(NY, 1, COLS), f32(1, ROWS)), gibbs, swap(row_parts, GROUP), scratch=(scale,)
     )
     (col_parts,) = call(relay_kernel, (f32(NZ, 1, COLS),), swap(col_parts, "y"))
     col_parts = swap(col_parts, "z")

time: 118 us -> 115 us (0.975)
  blocking collectives: 79.3 us -> 91.2 us
  starting transfers between devices: 25.1 us -> 15.8 us
  waiting for transfers between devices: 6.15 us -> 0.01 us
    all_gather x1, blocking collectives: 2.72 us -> 14.4 us  [local(): lax.all_gather(src_cells, GROUP)]
    ppermute x3 -> x0, starting transfers between devices: 9.32 us -> none  [local(): lax.ppermute(rows, 'x', [(i, (i + k) % NX) for i in range(NX)])]
    ppermute x3 -> x0, waiting for transfers between devices: 6.14 us -> none  [local(): lax.ppermute(rows, 'x', [(i, (i + k) % NX) for i in range(NX)])]
  transfers between devices with their start and end apart: 4 -> 1, of which waited for: 2 -> 0; matrix products, arithmetic and copies ran while one was open for 0% -> 0% of each run, Pallas kernels for 0% -> 0%
where the time goes in v5:
time: 115 us; the launch traced here: 114 us
  blocking collectives  91.2 us (79%)
  starting transfers between devices  15.8 us (14%)
  Pallas kernels  5.95 us (5%)
    all_to_all x6, blocking collectives, swap(): return lax.all_to_all(value, axes, 0, 0, tiled=True)  76.8 us
    all_to_all x1, starting transfers between devices, swap(): return lax.all_to_all(value, axes, 0, 0, tiled=True)  15.8 us
    all_gather x1, blocking collectives, local(): lax.all_gather(src_cells, GROUP)  14.4 us
    pallas_call x9, Pallas kernels, call(): pl.pallas_call(kernel, out_shape=outs, in_specs=[pl.BlockSpec(memory_spac...  5.95 us
  transfers between devices with their start and end apart: 1, of which 0 were waited for; matrix products, arithmetic and copies ran while one was open for 0% of the time, Pallas kernels for 0%

profile of v5, /device:TPU:1, one launch (start us, length us, event | category | flops | bytes accessed | tf_op | source)
XLA Modules:
  0.0 114.3 jit_solution(17418626292408894256)
XLA Ops:
  0.6 1.5 %shard_map.60 = f32[416,128]{1,0:T(8,128)} custom-call(f32[50,512]{1,0:T(8,128)} %tgt_ref.1, f32[4,128]{1,0:T(4,128)} %bitcast.9), custom_call_target="tpu_custom_call" | custom-call | tf_op jit(solution)/shard_map/pallas_call | solution.py:206
  2.2 15.8 %all-to-all-start = ((f32[16,1,3328]{2,1,0:T(1,128)}), f32[16,1,3328]{2,1,0:T(1,128)S(1)}, u32[]{:S(2)}, u32[]{:S(2)}) async-start(f32[16,1,3328]{2,1,0:T(1,128)} %bitcast.11), calls=%async_computation | async-start | bytes 425984 | tf_op jit(solution)/shard_map/all_to_all | solution.py:217
  17.9 14.4 %all-gather.1.rows_ref = f32[8,50,256]{2,1,0:T(8,128)S(1)} all-gather(f32[1,50,256]{2,1,0:T(8,128)} %bitcast.12), channel_id=2, replica_groups=mesh['y'=4,'x'=4,'core'=2,'z'=16] {'x','core'}, dimensions={0}, use_global_device_ids=true | all-gather | bytes 460800 | tf_op jit(solution)/shard_map/all_gather | solution.py:235
  32.3 0.0 copy-start
  32.3 0.7 copy-done
  33.0 0.2 shard_map.59
  33.2 0.0 all-to-all-done
  33.2 1.5 %shard_map.61 = (f32[1024,2048]{1,0:T(8,128)S(1)}, f32[8,1,2304]{2,1,0:T(1,128)S(1)}, f32[1,1024]{1,0:T(1,128)S(1)}) custom-call(bf16[256,2048]{1,0:T(8,128)(2,1)S(1)} %get-tuple-element.11.x_ref, f32[416,128]{1,0:T(8,128)S(1)} %bitcast.7, f32[1,256]{1,0:T(1,128)S(1)} %get-tuple-element.12.mass_ref), custom_call_target="tpu_custom_call" | custom-call | tf_op jit(solution)/shard_map/pallas_call | solution.py:206
  34.8 11.6 %all_to_all.35.parts_ref = f32[8,1,2304]{2,1,0:T(1,128)S(1)} all-to-all(f32[8,1,2304]{2,1,0:T(1,128)S(1)} %get-tuple-element.14), channel_id=1, replica_groups=mesh['y'=4,'x'=4,'core'=2,'z'=16] {'x','core'}, dimensions={0} | all-to-all | bytes 147456 | tf_op jit(solution)/shard_map/all_to_all | solution.py:217
  46.3 0.6 shard_map.62
  47.0 8.2 %all_to_all.36.parts_ref = f32[4,1,1024]{2,1,0:T(1,128)S(1)} all-to-all(f32[4,1,1024]{2,1,0:T(1,128)S(1)} %get-tuple-element.15), channel_id=1, replica_groups=mesh['y'=4,'x'=4,'core'=2,'z'=16] {'y'}, dimensions={0} | all-to-all | bytes 32768 | tf_op jit(solution)/shard_map/all_to_all | solution.py:217
  55.2 20.1 %all_to_all.37.parts_ref = f32[16,1,1024]{2,1,0:T(1,128)S(1)} all-to-all(f32[16,1,1024]{2,1,0:T(1,128)S(1)} %shard_map.63), channel_id=1, replica_groups=mesh['y'=4,'x'=4,'core'=2,'z'=16] {'z'}, dimensions={0} | all-to-all | bytes 131072 | tf_op jit(solution)/shard_map/all_to_all | solution.py:217
  75.2 0.0 copy-start.1
  75.2 0.7 shard_map.64
  75.9 11.0 %all_to_all.38.parts_ref = f32[8,1,2048]{2,1,0:T(1,128)S(1)} all-to-all(f32[8,1,2048]{2,1,0:T(1,128)S(1)} %shard_map.64), channel_id=1, replica_groups=mesh['y'=4,'x'=4,'core'=2,'z'=16] {'x','core'}, dimensions={0} | all-to-all | bytes 131072 | tf_op jit(solution)/shard_map/all_to_all | solution.py:217
  86.9 0.7 shard_map.65
  87.6 13.8 %all_to_all.39.landed_ref = f32[16,1,384]{2,1,0:T(1,128)S(1)} all-to-all(f32[16,1,384]{2,1,0:T(1,128)S(1)} %shard_map.65), channel_id=1, replica_groups=mesh['y'=4,'x'=4,'core'=2,'z'=16] {'z'}, dimensions={0} | all-to-all | bytes 49152 | tf_op jit(solution)/shard_map/all_to_all | solution.py:217
  101.5 12.1 %all_to_all.40.parts_ref = f32[32,1,128]{2,1,0:T(1,128)S(1)} all-to-all(f32[32,1,128]{2,1,0:T(1,128)S(1)} %shard_map.66), channel_id=1, replica_groups=mesh['y'=4,'x'=4,'core'=2,'z'=16] {'y','x','core'}, dimensions={0} | all-to-all | bytes 32768 | tf_op jit(solution)/shard_map/all_to_all | solution.py:217
  113.6 0.0 copy-done.1
  113.6 0.7 shard_map.67
  (2 shorter events, 0.0 us)
Async XLA Ops:
  2.2 31.1 %all-to-all-start = ((f32[16,1,3328]{2,1,0:T(1,128)}), f32[16,1,3328]{2,1,0:T(1,128)S(1)}, u32[]{:S(2)}, u32[]{:S(2)}) async-start(f32[16,1,3328]{2,1,0:T(1,128)} %bitcast.11), calls=%async_computation | async-start | bytes 425984 | tf_op jit(solution)/shard_map/all_to_all | solution.py:217
  32.3 0.7 copy-start
  75.2 38.4 %copy-start.1 = (f32[512]{0:T(512)S(1)}, f32[512]{0:T(512)}, u32[]{:S(2)}) copy-start(f32[512]{0:T(512)} %param.7) | copy-start | bytes 6148

commit v6 on v5

--- a/solution.py
+++ b/solution.py
@@ -15,6 +15,7 @@
 ROWS, COLS = 2048, 1024
 PIECE = 64
 OWN = 256
+ORDER = [(8 - k) % NZ for k in range(NZ)]
 EPS = 2.0
 FULL = 60 << 20
 
@@ -158,7 +159,7 @@
     own = scale_ref[:, pl.ds(pl.multiple_of(me * OWN, OWN), OWN)]
     for j in range(COLS // 128):
         total = columns(gibbs_ref, scale_ref, j)
-        for k in (2 * j, 2 * j + 1):
+        for k in (ORDER[2 * j], ORDER[2 * j + 1]):
             leaving_ref[k, :, 0:OWN] = own
             leaving_ref[k, :, OWN : OWN + 128] = total
             total = pltpu.roll(total, PIECE, 1)
@@ -213,8 +214,8 @@
     )(*args)
 
 
-def swap(value, axes):
-    return lax.all_to_all(value, axes, 0, 0, tiled=True)
+def swap(value, axes, groups=None):
+    return lax.all_to_all(value, axes, 0, 0, tiled=True, axis_index_groups=groups)
 
 
 def local(src_cells, tgt_cells, src_mass, tgt_mass):
@@ -228,7 +229,7 @@
         space=pltpu.HBM,
         limit=60 << 20,
     )
-    cols = swap(cols.reshape(NZ, 1, HALF * 128), "z").reshape(NZ * HALF, 128)
+    cols = swap(cols.reshape(NZ, 1, HALF * 128), "z", [ORDER]).reshape(NZ * HALF, 128)
     stack, own_mass = call(
         stack_kernel,
         (jax.ShapeDtypeStruct((256, ROWS), jnp.bfloat16), f32(1, OWN)),

time: 115 us -> 113 us (0.983)
  blocking collectives: 91.2 us -> 86.1 us
  starting transfers between devices: 15.8 us -> 19.1 us
    all_to_all x6, blocking collectives: 76.8 us -> 71.4 us  [swap(): lax.all_to_all(value, axes, 0, 0, tiled=True, axis_index_groups=groups)]
    all_to_all x1, starting transfers between devices: 15.8 us -> 19.1 us  [swap(): lax.all_to_all(value, axes, 0, 0, tiled=True, axis_index_groups=groups)]
where the time goes in v6:
time: 113 us
  blocking collectives  86.1 us (76%)
  starting transfers between devices  19.1 us (17%)
  Pallas kernels  5.95 us (5%)
    all_to_all x6, blocking collectives, swap(): lax.all_to_all(value, axes, 0, 0, tiled=True, axis_index_groups=groups)  71.4 us
    all_to_all x1, starting transfers between devices, swap(): lax.all_to_all(value, axes, 0, 0, tiled=True, axis_index_groups=groups)  19.1 us
    all_gather x1, blocking collectives, local(): lax.all_gather(src_cells, GROUP)  14.7 us
    pallas_call x9, Pallas kernels, call(): pl.pallas_call(kernel, out_shape=outs, in_specs=[pl.BlockSpec(memory_spac...  5.95 us
  transfers between devices with their start and end apart: 1, of which 0 were waited for; matrix products, arithmetic and copies ran while one was open for 0% of the time, Pallas kernels for 0%

profile of v6, /device:TPU:1, one launch (start us, length us, event | category | flops | bytes accessed | tf_op | source)
XLA Modules:
  0.0 112.5 jit_solution(11719520571594958623)
XLA Ops:
  0.6 1.5 %shard_map.60 = f32[416,128]{1,0:T(8,128)} custom-call(f32[50,512]{1,0:T(8,128)} %tgt_ref.1, f32[4,128]{1,0:T(4,128)} %bitcast.9), custom_call_target="tpu_custom_call" | custom-call | tf_op jit(solution)/shard_map/pallas_call | solution.py:207
  2.2 19.1 %all-to-all-start = ((f32[16,1,3328]{2,1,0:T(1,128)}), f32[16,1,3328]{2,1,0:T(1,128)S(1)}, u32[]{:S(2)}, u32[]{:S(2)}) async-start(f32[16,1,3328]{2,1,0:T(1,128)} %bitcast.11), calls=%async_computation | async-start | bytes 425984 | tf_op jit(solution)/shard_map/all_to_all | solution.py:218
  21.3 14.7 %all-gather.1.rows_ref = f32[8,50,256]{2,1,0:T(8,128)S(1)} all-gather(f32[1,50,256]{2,1,0:T(8,128)} %bitcast.12), channel_id=2, replica_groups=mesh['y'=4,'x'=4,'core'=2,'z'=16] {'x','core'}, dimensions={0}, use_global_device_ids=true | all-gather | bytes 460800 | tf_op jit(solution)/shard_map/all_gather | solution.py:236
  36.0 0.0 copy-start
  36.0 0.7 copy-done
  36.7 0.2 shard_map.59
  36.8 0.0 all-to-all-done
  36.9 1.5 %shard_map.61 = (f32[1024,2048]{1,0:T(8,128)S(1)}, f32[8,1,2304]{2,1,0:T(1,128)S(1)}, f32[1,1024]{1,0:T(1,128)S(1)}) custom-call(bf16[256,2048]{1,0:T(8,128)(2,1)S(1)} %get-tuple-element.11.x_ref, f32[416,128]{1,0:T(8,128)S(1)} %bitcast.7, f32[1,256]{1,0:T(1,128)S(1)} %get-tuple-element.12.mass_ref), custom_call_target="tpu_custom_call" | custom-call | tf_op jit(solution)/shard_map/pallas_call | solution.py:207
  38.4 8.5 %all_to_all.35.parts_ref = f32[8,1,2304]{2,1,0:T(1,128)S(1)} all-to-all(f32[8,1,2304]{2,1,0:T(1,128)S(1)} %get-tuple-element.14), channel_id=1, replica_groups=mesh['y'=4,'x'=4,'core'=2,'z'=16] {'x','core'}, dimensions={0} | all-to-all | bytes 147456 | tf_op jit(solution)/shard_map/all_to_all | solution.py:218
  46.9 0.6 shard_map.62
  47.6 8.2 %all_to_all.36.parts_ref = f32[4,1,1024]{2,1,0:T(1,128)S(1)} all-to-all(f32[4,1,1024]{2,1,0:T(1,128)S(1)} %get-tuple-element.15), channel_id=1, replica_groups=mesh['y'=4,'x'=4,'core'=2,'z'=16] {'y'}, dimensions={0} | all-to-all | bytes 32768 | tf_op jit(solution)/shard_map/all_to_all | solution.py:218
  55.8 17.7 %all_to_all.37.parts_ref = f32[16,1,1024]{2,1,0:T(1,128)S(1)} all-to-all(f32[16,1,1024]{2,1,0:T(1,128)S(1)} %shard_map.63), channel_id=1, replica_groups=mesh['y'=4,'x'=4,'core'=2,'z'=16] {'z'}, dimensions={0} | all-to-all | bytes 131072 | tf_op jit(solution)/shard_map/all_to_all | solution.py:218
  73.5 0.0 copy-start.1
  73.5 0.7 shard_map.64
  74.2 11.0 %all_to_all.38.parts_ref = f32[8,1,2048]{2,1,0:T(1,128)S(1)} all-to-all(f32[8,1,2048]{2,1,0:T(1,128)S(1)} %shard_map.64), channel_id=1, replica_groups=mesh['y'=4,'x'=4,'core'=2,'z'=16] {'x','core'}, dimensions={0} | all-to-all | bytes 131072 | tf_op jit(solution)/shard_map/all_to_all | solution.py:218
  85.2 0.7 shard_map.65
  85.9 13.8 %all_to_all.39.landed_ref = f32[16,1,384]{2,1,0:T(1,128)S(1)} all-to-all(f32[16,1,384]{2,1,0:T(1,128)S(1)} %shard_map.65), channel_id=1, replica_groups=mesh['y'=4,'x'=4,'core'=2,'z'=16] {'z'}, dimensions={0} | all-to-all | bytes 49152 | tf_op jit(solution)/shard_map/all_to_all | solution.py:218
  99.8 12.1 %all_to_all.40.parts_ref = f32[32,1,128]{2,1,0:T(1,128)S(1)} all-to-all(f32[32,1,128]{2,1,0:T(1,128)S(1)} %shard_map.66), channel_id=1, replica_groups=mesh['y'=4,'x'=4,'core'=2,'z'=16] {'y','x','core'}, dimensions={0} | all-to-all | bytes 32768 | tf_op jit(solution)/shard_map/all_to_all | solution.py:218
  111.9 0.0 copy-done.1
  111.9 0.7 shard_map.67
  (2 shorter events, 0.0 us)
Async XLA Ops:
  2.2 34.7 %all-to-all-start = ((f32[16,1,3328]{2,1,0:T(1,128)}), f32[16,1,3328]{2,1,0:T(1,128)S(1)}, u32[]{:S(2)}, u32[]{:S(2)}) async-start(f32[16,1,3328]{2,1,0:T(1,128)} %bitcast.11), calls=%async_computation | async-start | bytes 425984 | tf_op jit(solution)/shard_map/all_to_all | solution.py:218
  36.0 0.7 copy-start
  73.5 38.4 %copy-start.1 = (f32[512]{0:T(512)S(1)}, f32[512]{0:T(512)}, u32[]{:S(2)}) copy-start(f32[512]{0:T(512)} %param.7) | copy-start | bytes 6148

commit v7 on v6

--- a/solution.py
+++ b/solution.py
@@ -15,7 +15,7 @@
 ROWS, COLS = 2048, 1024
 PIECE = 64
 OWN = 256
-ORDER = [(8 - k) % NZ for k in range(NZ)]
+ORDER = [(12 - k) % NZ for k in range(NZ)]
 EPS = 2.0
 FULL = 60 << 20
 

time: 113 us -> 110 us (0.973)
  starting transfers between devices: 19.1 us -> 16 us
    all_to_all x1, starting transfers between devices: 19.1 us -> 16 us  [swap(): lax.all_to_all(value, axes, 0, 0, tiled=True, axis_index_groups=groups)]
where the time goes in v7:
time: 110 us
  blocking collectives  86.6 us (79%)
  starting transfers between devices  16 us (15%)
  Pallas kernels  5.95 us (5%)
    all_to_all x6, blocking collectives, swap(): lax.all_to_all(value, axes, 0, 0, tiled=True, axis_index_groups=groups)  71.9 us
    all_to_all x1, starting transfers between devices, swap(): lax.all_to_all(value, axes, 0, 0, tiled=True, axis_index_groups=groups)  16 us
    all_gather x1, blocking collectives, local(): lax.all_gather(src_cells, GROUP)  14.7 us
    pallas_call x9, Pallas kernels, call(): pl.pallas_call(kernel, out_shape=outs, in_specs=[pl.BlockSpec(memory_spac...  5.95 us
  transfers between devices with their start and end apart: 1, of which 0 were waited for; matrix products, arithmetic and copies ran while one was open for 0% of the time, Pallas kernels for 0%

profile of v7, /device:TPU:1, one launch (start us, length us, event | category | flops | bytes accessed | tf_op | source)
XLA Modules:
  0.0 109.9 jit_solution(2670290645565927453)
XLA Ops:
  0.6 1.5 %shard_map.60 = f32[416,128]{1,0:T(8,128)} custom-call(f32[50,512]{1,0:T(8,128)} %tgt_ref.1, f32[4,128]{1,0:T(4,128)} %bitcast.9), custom_call_target="tpu_custom_call" | custom-call | tf_op jit(solution)/shard_map/pallas_call | solution.py:207
  2.2 16.0 %all-to-all-start = ((f32[16,1,3328]{2,1,0:T(1,128)}), f32[16,1,3328]{2,1,0:T(1,128)S(1)}, u32[]{:S(2)}, u32[]{:S(2)}) async-start(f32[16,1,3328]{2,1,0:T(1,128)} %bitcast.11), calls=%async_computation | async-start | bytes 425984 | tf_op jit(solution)/shard_map/all_to_all | solution.py:218
  18.1 14.7 %all-gather.1.rows_ref = f32[8,50,256]{2,1,0:T(8,128)S(1)} all-gather(f32[1,50,256]{2,1,0:T(8,128)} %bitcast.12), channel_id=2, replica_groups=mesh['y'=4,'x'=4,'core'=2,'z'=16] {'x','core'}, dimensions={0}, use_global_device_ids=true | all-gather | bytes 460800 | tf_op jit(solution)/shard_map/all_gather | solution.py:236
  32.8 0.0 copy-start
  32.8 0.7 copy-done
  33.5 0.2 shard_map.59
  33.7 0.0 all-to-all-done
  33.7 1.5 %shard_map.61 = (f32[1024,2048]{1,0:T(8,128)S(1)}, f32[8,1,2304]{2,1,0:T(1,128)S(1)}, f32[1,1024]{1,0:T(1,128)S(1)}) custom-call(bf16[256,2048]{1,0:T(8,128)(2,1)S(1)} %get-tuple-element.11.x_ref, f32[416,128]{1,0:T(8,128)S(1)} %bitcast.7, f32[1,256]{1,0:T(1,128)S(1)} %get-tuple-element.12.mass_ref), custom_call_target="tpu_custom_call" | custom-call | tf_op jit(solution)/shard_map/pallas_call | solution.py:207
  35.2 8.8 %all_to_all.35.parts_ref = f32[8,1,2304]{2,1,0:T(1,128)S(1)} all-to-all(f32[8,1,2304]{2,1,0:T(1,128)S(1)} %get-tuple-element.14), channel_id=1, replica_groups=mesh['y'=4,'x'=4,'core'=2,'z'=16] {'x','core'}, dimensions={0} | all-to-all | bytes 147456 | tf_op jit(solution)/shard_map/all_to_all | solution.py:218
  44.0 0.6 shard_map.62
  44.6 8.2 %all_to_all.36.parts_ref = f32[4,1,1024]{2,1,0:T(1,128)S(1)} all-to-all(f32[4,1,1024]{2,1,0:T(1,128)S(1)} %get-tuple-element.15), channel_id=1, replica_groups=mesh['y'=4,'x'=4,'core'=2,'z'=16] {'y'}, dimensions={0} | all-to-all | bytes 32768 | tf_op jit(solution)/shard_map/all_to_all | solution.py:218
  52.8 18.0 %all_to_all.37.parts_ref = f32[16,1,1024]{2,1,0:T(1,128)S(1)} all-to-all(f32[16,1,1024]{2,1,0:T(1,128)S(1)} %shard_map.63), channel_id=1, replica_groups=mesh['y'=4,'x'=4,'core'=2,'z'=16] {'z'}, dimensions={0} | all-to-all | bytes 131072 | tf_op jit(solution)/shard_map/all_to_all | solution.py:218
  70.8 0.0 copy-start.1
  70.8 0.7 shard_map.64
  71.5 11.0 %all_to_all.38.parts_ref = f32[8,1,2048]{2,1,0:T(1,128)S(1)} all-to-all(f32[8,1,2048]{2,1,0:T(1,128)S(1)} %shard_map.64), channel_id=1, replica_groups=mesh['y'=4,'x'=4,'core'=2,'z'=16] {'x','core'}, dimensions={0} | all-to-all | bytes 131072 | tf_op jit(solution)/shard_map/all_to_all | solution.py:218
  82.6 0.7 shard_map.65
  83.3 13.8 %all_to_all.39.landed_ref = f32[16,1,384]{2,1,0:T(1,128)S(1)} all-to-all(f32[16,1,384]{2,1,0:T(1,128)S(1)} %shard_map.65), channel_id=1, replica_groups=mesh['y'=4,'x'=4,'core'=2,'z'=16] {'z'}, dimensions={0} | all-to-all | bytes 49152 | tf_op jit(solution)/shard_map/all_to_all | solution.py:218
  97.1 12.1 %all_to_all.40.parts_ref = f32[32,1,128]{2,1,0:T(1,128)S(1)} all-to-all(f32[32,1,128]{2,1,0:T(1,128)S(1)} %shard_map.66), channel_id=1, replica_groups=mesh['y'=4,'x'=4,'core'=2,'z'=16] {'y','x','core'}, dimensions={0} | all-to-all | bytes 32768 | tf_op jit(solution)/shard_map/all_to_all | solution.py:218
  109.2 0.0 copy-done.1
  109.2 0.7 shard_map.67
  (2 shorter events, 0.0 us)
Async XLA Ops:
  2.2 31.5 %all-to-all-start = ((f32[16,1,3328]{2,1,0:T(1,128)}), f32[16,1,3328]{2,1,0:T(1,128)S(1)}, u32[]{:S(2)}, u32[]{:S(2)}) async-start(f32[16,1,3328]{2,1,0:T(1,128)} %bitcast.11), calls=%async_computation | async-start | bytes 425984 | tf_op jit(solution)/shard_map/all_to_all | solution.py:218
  32.8 0.7 copy-start
  70.8 38.4 %copy-start.1 = (f32[512]{0:T(512)S(1)}, f32[512]{0:T(512)}, u32[]{:S(2)}) copy-start(f32[512]{0:T(512)} %param.7) | copy-start | bytes 6148

commit v8 on v7

--- a/solution.py
+++ b/solution.py
@@ -15,7 +15,7 @@
 ROWS, COLS = 2048, 1024
 PIECE = 64
 OWN = 256
-ORDER = [(12 - k) % NZ for k in range(NZ)]
+ORDER = [(12 + 7 * k) % NZ for k in range(NZ)]
 EPS = 2.0
 FULL = 60 << 20
 
@@ -39,17 +39,22 @@
     return row, jnp.where(keep, cells, 0.0)
 
 
-def pack_kernel(tgt_ref, tgt_mass_ref, cols_ref, cells_ref, mass_ref, sems):
-    x, core = lax.axis_index("x"), lax.axis_index("core")
+def pack_kernel(tgt_ref, tgt_mass_ref, src_ref, src_mass_ref, cols_ref, rows_ref, cells_ref, mass_ref, src_buf, src_mass_buf, sems):
+    x, core, z = (lax.axis_index(name) for name in ("x", "core", "z"))
     here = pl.ds(pl.multiple_of(x * 128, 128), 128)
     copies = (
         pltpu.make_async_copy(tgt_ref.at[:, here], cells_ref, sems.at[0]),
         pltpu.make_async_copy(tgt_mass_ref, mass_ref, sems.at[1]),
+        pltpu.make_async_copy(src_ref, src_buf, sems.at[2]),
+        pltpu.make_async_copy(src_mass_ref, src_mass_buf, sems.at[3]),
     )
     for copy in copies:
         copy.start()
     for copy in copies:
         copy.wait()
+    rows_ref[0:PC] = src_buf[...]
+    for k in range(2):
+        rows_ref[PC : PC + 1, k * 128 : (k + 1) * 128] = src_mass_buf[pl.ds(2 * z + k, 1)]
     cells = cells_ref[...]
     top = cells[0:HALF]
     bottom = jnp.concatenate([cells[HALF:PC], mass_ref[pl.ds(x, 1)], jnp.zeros((1, 128), jnp.float32)], axis=0)
@@ -61,13 +66,11 @@
         cols_ref[k * HALF : (k + 1) * HALF] = piece
 
 
-def stack_kernel(rows_ref, mass_ref, x_ref, own_mass_ref):
-    z = lax.axis_index("z")
-    for k in range(2):
-        own_mass_ref[:, k * 128 : (k + 1) * 128] = mass_ref[pl.ds(2 * z + k, 1)]
+def stack_kernel(rows_ref, x_ref, row_mass_ref):
     for g in range(NG):
         here = slice(g * OWN, (g + 1) * OWN)
-        cells = rows_ref[g]
+        row_mass_ref[:, here] = rows_ref[g, PC : PC + 1]
+        cells = rows_ref[g, 0:PC]
         norm = -0.5 * jnp.sum(cells * cells, axis=0, keepdims=True)
         ones = jnp.ones((3, OWN), jnp.float32)
         high, low = split(cells)
@@ -83,9 +86,7 @@
         x_ref[192:256, here] = low
 
 
-def gibbs_kernel(x_ref, cols_ref, mass_ref, gibbs_ref, part_ref, col_mass_ref, y_ref):
-    for k in range(NG):
-        part_ref[k, :, ROWS : ROWS + OWN] = mass_ref[...]
+def gibbs_kernel(x_ref, cols_ref, gibbs_ref, part_ref, col_mass_ref, y_ref):
     lane = lax.broadcasted_iota(jnp.int32, (32, 128), 1)
     gap = jnp.zeros((32 - HALF, 128), jnp.float32)
     for t in range(NZ // 2):
@@ -134,13 +135,8 @@
     return jnp.sum(total.T, axis=0, keepdims=True)
 
 
-def column_kernel(gibbs_ref, parts_ref, part_ref, mass_ref, scale_ref):
-    for k in range(NG):
-        mass_ref[:, k * OWN : (k + 1) * OWN] = parts_ref[k, :, ROWS : ROWS + OWN]
-    total = parts_ref[0, :, 0:ROWS]
-    for k in range(1, NG):
-        total = total + parts_ref[k, :, 0:ROWS]
-    scale_ref[...] = mass_ref[...] / total
+def column_kernel(gibbs_ref, parts_ref, mass_ref, part_ref, scale_ref):
+    scale_ref[...] = mass_ref[...] / summed(parts_ref)
     for j in range(COLS // 128):
         total = columns(gibbs_ref, scale_ref, j)
         for k in range(NY):
@@ -220,33 +216,34 @@
 
 def local(src_cells, tgt_cells, src_mass, tgt_mass):
     tgt_mass = tgt_mass.reshape(NX, 128)
-    (cols,) = call(
+    cols, rows = call(
         pack_kernel,
-        (f32(NZ * HALF, 128),),
+        (f32(NZ * HALF, 128), f32(PC + 1, OWN)),
         tgt_cells,
         tgt_mass,
-        scratch=[pltpu.VMEM((PC, 128), jnp.float32), pltpu.VMEM((NX, 128), jnp.float32), pltpu.SemaphoreType.DMA((2,))],
+        src_cells,
+        src_mass.reshape(NZ * 2, 128),
+        scratch=[pltpu.VMEM(shape, jnp.float32) for shape in ((PC, 128), (NX, 128), (PC, OWN), (NZ * 2, 128))]
+        + [pltpu.SemaphoreType.DMA((4,))],
         space=pltpu.HBM,
         limit=60 << 20,
     )
     cols = swap(cols.reshape(NZ, 1, HALF * 128), "z", [ORDER]).reshape(NZ * HALF, 128)
-    stack, own_mass = call(
+    stack, row_mass = call(
         stack_kernel,
-        (jax.ShapeDtypeStruct((256, ROWS), jnp.bfloat16), f32(1, OWN)),
-        lax.all_gather(src_cells, GROUP),
-        src_mass.reshape(NZ * 2, 128),
+        (jax.ShapeDtypeStruct((256, ROWS), jnp.bfloat16), f32(1, ROWS)),
+        lax.all_gather(rows, GROUP),
     )
     gibbs, row_parts, col_mass = call(
         gibbs_kernel,
-        (f32(COLS, ROWS), f32(NG, 1, ROWS + OWN), f32(1, COLS)),
+        (f32(COLS, ROWS), f32(NG, 1, ROWS), f32(1, COLS)),
         stack,
         cols,
-        own_mass,
         scratch=(pltpu.VMEM((COLS, 256), jnp.bfloat16),),
     )
     scale = pltpu.VMEM((1, ROWS), jnp.float32)
-    col_parts, row_mass = call(
-        column_kernel, (f32(NY, 1, COLS), f32(1, ROWS)), gibbs, swap(row_parts, GROUP), scratch=(scale,)
+    (col_parts,) = call(
+        column_kernel, (f32(NY, 1, COLS),), gibbs, swap(row_parts, GROUP), row_mass, scratch=(scale,)
     )
     (col_parts,) = call(relay_kernel, (f32(NZ, 1, COLS),), swap(col_parts, "y"))
     col_parts = swap(col_parts, "z")

time: 110 us -> 111 us (level)
  no operation moved by 1% of the time
where the time goes in v8:
time: 111 us; the launch traced here: 110 us
  blocking collectives  87.3 us (79%)
  starting transfers between devices  16 us (14%)
  Pallas kernels  6.12 us (6%)
    all_to_all x6, blocking collectives, swap(): lax.all_to_all(value, axes, 0, 0, tiled=True, axis_index_groups=groups)  72.6 us
    all_to_all x1, starting transfers between devices, swap(): lax.all_to_all(value, axes, 0, 0, tiled=True, axis_index_groups=groups)  16 us
    all_gather x1, blocking collectives, local(): lax.all_gather(rows, GROUP)  14.7 us
    pallas_call x9, Pallas kernels, call(): pl.pallas_call(kernel, out_shape=outs, in_specs=[pl.BlockSpec(memory_spac...  6.12 us
  transfers between devices with their start and end apart: 1, of which 0 were waited for; matrix products, arithmetic and copies ran while one was open for 0% of the time, Pallas kernels for 0%

profile of v8, /device:TPU:1, one launch (start us, length us, event | category | flops | bytes accessed | tf_op | source)
XLA Modules:
  0.0 110.0 jit_solution(5261477725371911895)
XLA Ops:
  0.6 1.7 %shard_map.59 = (f32[416,128]{1,0:T(8,128)}, f32[51,256]{1,0:T(8,128)}) custom-call(f32[50,512]{1,0:T(8,128)} %tgt_ref.1, f32[4,128]{1,0:T(4,128)} %bitcast.8, f32[50,256]{1,0:T(8,128)} %src_ref.1, f32[32,128]{1,0:T(8,128)} %bitcast.12), custom_call_target="tpu_custom_call" | custom-call | tf_op jit(solution)/shard_map/pallas_call | solution.py:203
  2.3 16.0 %all-to-all-start = ((f32[16,1,3328]{2,1,0:T(1,128)}), f32[16,1,3328]{2,1,0:T(1,128)S(1)}, u32[]{:S(2)}, u32[]{:S(2)}) async-start(f32[16,1,3328]{2,1,0:T(1,128)} %bitcast.10), calls=%async_computation | async-start | bytes 425984 | tf_op jit(solution)/shard_map/all_to_all | solution.py:214
  18.3 14.7 %all-gather.1.rows_ref = f32[8,51,256]{2,1,0:T(8,128)S(1)} all-gather(f32[1,51,256]{2,1,0:T(8,128)} %bitcast.11), channel_id=2, replica_groups=mesh['y'=4,'x'=4,'core'=2,'z'=16] {'x','core'}, dimensions={0}, use_global_device_ids=true | all-gather | bytes 470016 | tf_op jit(solution)/shard_map/all_gather | solution.py:235
  32.9 0.2 shard_map.60
  33.1 0.0 all-to-all-done
  33.1 1.5 %shard_map.61 = (f32[1024,2048]{1,0:T(8,128)S(1)}, f32[8,1,2048]{2,1,0:T(1,128)S(1)}, f32[1,1024]{1,0:T(1,128)S(1)}) custom-call(bf16[256,2048]{1,0:T(8,128)(2,1)S(1)} %get-tuple-element.12.x_ref, f32[416,128]{1,0:T(8,128)S(1)} %bitcast.7), custom_call_target="tpu_custom_call" | custom-call | tf_op jit(solution)/shard_map/pallas_call | solution.py:203
  34.7 9.5 %all_to_all.35.parts_ref = f32[8,1,2048]{2,1,0:T(1,128)S(1)} all-to-all(f32[8,1,2048]{2,1,0:T(1,128)S(1)} %get-tuple-element.15), channel_id=1, replica_groups=mesh['y'=4,'x'=4,'core'=2,'z'=16] {'x','core'}, dimensions={0} | all-to-all | bytes 131072 | tf_op jit(solution)/shard_map/all_to_all | solution.py:214
  44.1 0.6 shard_map.62
  44.8 8.2 %all_to_all.36.parts_ref = f32[4,1,1024]{2,1,0:T(1,128)S(1)} all-to-all(f32[4,1,1024]{2,1,0:T(1,128)S(1)} %shard_map.62), channel_id=1, replica_groups=mesh['y'=4,'x'=4,'core'=2,'z'=16] {'y'}, dimensions={0} | all-to-all | bytes 32768 | tf_op jit(solution)/shard_map/all_to_all | solution.py:214
  53.0 18.1 %all_to_all.37.parts_ref = f32[16,1,1024]{2,1,0:T(1,128)S(1)} all-to-all(f32[16,1,1024]{2,1,0:T(1,128)S(1)} %shard_map.63), channel_id=1, replica_groups=mesh['y'=4,'x'=4,'core'=2,'z'=16] {'z'}, dimensions={0} | all-to-all | bytes 131072 | tf_op jit(solution)/shard_map/all_to_all | solution.py:214
  71.1 0.0 copy-start
  71.1 0.7 shard_map.64
  71.8 10.9 %all_to_all.38.parts_ref = f32[8,1,2048]{2,1,0:T(1,128)S(1)} all-to-all(f32[8,1,2048]{2,1,0:T(1,128)S(1)} %shard_map.64), channel_id=1, replica_groups=mesh['y'=4,'x'=4,'core'=2,'z'=16] {'x','core'}, dimensions={0} | all-to-all | bytes 131072 | tf_op jit(solution)/shard_map/all_to_all | solution.py:214
  82.7 0.7 shard_map.65
  83.4 13.8 %all_to_all.39.landed_ref = f32[16,1,384]{2,1,0:T(1,128)S(1)} all-to-all(f32[16,1,384]{2,1,0:T(1,128)S(1)} %shard_map.65), channel_id=1, replica_groups=mesh['y'=4,'x'=4,'core'=2,'z'=16] {'z'}, dimensions={0} | all-to-all | bytes 49152 | tf_op jit(solution)/shard_map/all_to_all | solution.py:214
  97.3 12.1 %all_to_all.40.parts_ref = f32[32,1,128]{2,1,0:T(1,128)S(1)} all-to-all(f32[32,1,128]{2,1,0:T(1,128)S(1)} %shard_map.66), channel_id=1, replica_groups=mesh['y'=4,'x'=4,'core'=2,'z'=16] {'y','x','core'}, dimensions={0} | all-to-all | bytes 32768 | tf_op jit(solution)/shard_map/all_to_all | solution.py:214
  109.4 0.0 copy-done
  109.4 0.7 shard_map.67
  (2 shorter events, 0.0 us)
Async XLA Ops:
  2.3 30.8 %all-to-all-start = ((f32[16,1,3328]{2,1,0:T(1,128)}), f32[16,1,3328]{2,1,0:T(1,128)S(1)}, u32[]{:S(2)}, u32[]{:S(2)}) async-start(f32[16,1,3328]{2,1,0:T(1,128)} %bitcast.10), calls=%async_computation | async-start | bytes 425984 | tf_op jit(solution)/shard_map/all_to_all | solution.py:214
  71.1 38.3 %copy-start = (f32[512]{0:T(512)S(1)}, f32[512]{0:T(512)}, u32[]{:S(2)}) copy-start(f32[512]{0:T(512)} %param.7) | copy-start | bytes 6148

commit v9 on v7

--- a/solution.py
+++ b/solution.py
@@ -20,12 +20,6 @@
 FULL = 60 << 20
 
 
-def split(value):
-    high = value.astype(jnp.bfloat16)
-    low = (value - high.astype(jnp.float32)).astype(jnp.bfloat16)
-    return high, low
-
-
 def pieces(norm):
     first = norm.astype(jnp.bfloat16).astype(jnp.float32)
     rest = norm - first
@@ -70,17 +64,17 @@
         cells = rows_ref[g]
         norm = -0.5 * jnp.sum(cells * cells, axis=0, keepdims=True)
         ones = jnp.ones((3, OWN), jnp.float32)
-        high, low = split(cells)
-        high = high.astype(jnp.float32)
-        low = low.astype(jnp.float32)
+        high, mid, low = pieces(cells)
         gap = jnp.zeros((8, OWN), jnp.float32)
         plus = jnp.concatenate([high[0:HALF], *pieces(norm), ones, high[HALF:PC], gap], axis=0)
-        low = jnp.concatenate([low[0:HALF], gap[0:6], low[HALF:PC], gap], axis=0).astype(jnp.bfloat16)
         row = lax.broadcasted_iota(jnp.int32, (64, OWN), 0)
-        x_ref[0:64, here] = plus.astype(jnp.bfloat16)
-        x_ref[64:128, here] = jnp.where((row < HALF) | (row >= 32), plus, 0.0).astype(jnp.bfloat16)
-        x_ref[128:192, here] = low
-        x_ref[192:256, here] = low
+        high = jnp.where((row < HALF) | (row >= 32), plus, 0.0).astype(jnp.bfloat16)
+        mid, low = (
+            jnp.concatenate([part[0:HALF], gap[0:6], part[HALF:PC], gap], axis=0).astype(jnp.bfloat16)
+            for part in (mid, low)
+        )
+        for k, part in enumerate((plus.astype(jnp.bfloat16), high, mid, mid, high, low)):
+            x_ref[64 * k : 64 * (k + 1), here] = part
 
 
 def gibbs_kernel(x_ref, cols_ref, mass_ref, gibbs_ref, part_ref, col_mass_ref, y_ref):
@@ -98,13 +92,13 @@
         col_mass_ref[:, here] = bottom[MASS - 32 : MASS - 31]
         row, cells = masked(jnp.concatenate([top, bottom], axis=0))
         first, second, third = pieces(-0.5 * jnp.sum(cells * cells, axis=0, keepdims=True))
-        high, low = split(cells)
+        high, mid, low = pieces(cells)
         extra = jnp.where(row == 29, first, jnp.where(row == 30, second, jnp.where(row == 31, third, 0.0)))
         extra = jnp.where((row >= 26) & (row < 29), 1.0, extra)
-        both = jnp.concatenate([high.astype(jnp.float32) + extra, low.astype(jnp.float32)], axis=0)
-        turned = both.T.astype(jnp.bfloat16)
+        turned = jnp.concatenate([high + extra, mid], axis=0).T.astype(jnp.bfloat16)
         y_ref[here, 0:128] = turned
         y_ref[here, 128:256] = turned
+        y_ref[here, 256:384] = jnp.concatenate([low, high], axis=0).T.astype(jnp.bfloat16)
     for n in range(ROWS // 256):
         there = slice(n * 256, (n + 1) * 256)
         total = jnp.zeros((8, 256), jnp.float32)
@@ -232,7 +226,7 @@
     cols = swap(cols.reshape(NZ, 1, HALF * 128), "z", [ORDER]).reshape(NZ * HALF, 128)
     stack, own_mass = call(
         stack_kernel,
-        (jax.ShapeDtypeStruct((256, ROWS), jnp.bfloat16), f32(1, OWN)),
+        (jax.ShapeDtypeStruct((384, ROWS), jnp.bfloat16), f32(1, OWN)),
         lax.all_gather(src_cells, GROUP),
         src_mass.reshape(NZ * 2, 128),
     )
@@ -242,7 +236,7 @@
         stack,
         cols,
         own_mass,
-        scratch=(pltpu.VMEM((COLS, 256), jnp.bfloat16),),
+        scratch=(pltpu.VMEM((COLS, 384), jnp.bfloat16),),
     )
     scale = pltpu.VMEM((1, ROWS), jnp.float32)
     col_parts, row_mass = call(

time: 110 us -> 112 us (1.018)
  Pallas kernels: 5.95 us -> 7.15 us
    pallas_call x9, Pallas kernels: 5.95 us -> 7.15 us  [call(): pl.pallas_call(kernel, out_shape=outs, in_specs=[pl.BlockSpec(memory_spac...]
where the time goes in v9:
time: 112 us; the launch traced here: 111 us
  blocking collectives  86.5 us (77%)
  starting transfers between devices  16 us (14%)
  Pallas kernels  7.15 us (6%)
    all_to_all x6, blocking collectives, swap(): lax.all_to_all(value, axes, 0, 0, tiled=True, axis_index_groups=groups)  71.9 us
    all_to_all x1, starting transfers between devices, swap(): lax.all_to_all(value, axes, 0, 0, tiled=True, axis_index_groups=groups)  16 us
    all_gather x1, blocking collectives, local(): lax.all_gather(src_cells, GROUP)  14.7 us
    pallas_call x9, Pallas kernels, call(): pl.pallas_call(kernel, out_shape=outs, in_specs=[pl.BlockSpec(memory_spac...  7.15 us
  transfers between devices with their start and end apart: 1, of which 0 were waited for; matrix products, arithmetic and copies ran while one was open for 0% of the time, Pallas kernels for 0%

profile of v9, /device:TPU:1, one launch (start us, length us, event | category | flops | bytes accessed | tf_op | source)
XLA Modules:
  0.0 111.0 jit_solution(12130230422105449519)
XLA Ops:
  0.6 1.5 %shard_map.60 = f32[416,128]{1,0:T(8,128)} custom-call(f32[50,512]{1,0:T(8,128)} %tgt_ref.1, f32[4,128]{1,0:T(4,128)} %bitcast.9), custom_call_target="tpu_custom_call" | custom-call | tf_op jit(solution)/shard_map/pallas_call | solution.py:201
  2.2 16.0 %all-to-all-start = ((f32[16,1,3328]{2,1,0:T(1,128)}), f32[16,1,3328]{2,1,0:T(1,128)S(1)}, u32[]{:S(2)}, u32[]{:S(2)}) async-start(f32[16,1,3328]{2,1,0:T(1,128)} %bitcast.11), calls=%async_computation | async-start | bytes 425984 | tf_op jit(solution)/shard_map/all_to_all | solution.py:212
  18.1 14.7 %all-gather.1.rows_ref = f32[8,50,256]{2,1,0:T(8,128)S(1)} all-gather(f32[1,50,256]{2,1,0:T(8,128)} %bitcast.12), channel_id=2, replica_groups=mesh['y'=4,'x'=4,'core'=2,'z'=16] {'x','core'}, dimensions={0}, use_global_device_ids=true | all-gather | bytes 460800 | tf_op jit(solution)/shard_map/all_gather | solution.py:230
  32.8 0.0 copy-start
  32.8 0.7 copy-done
  33.5 0.2 shard_map.59
  33.7 0.0 all-to-all-done
  33.8 2.7 %shard_map.61 = (f32[1024,2048]{1,0:T(8,128)S(1)}, f32[8,1,2304]{2,1,0:T(1,128)S(1)}, f32[1,1024]{1,0:T(1,128)S(1)}) custom-call(bf16[384,2048]{1,0:T(8,128)(2,1)S(1)} %get-tuple-element.11.x_ref, f32[416,128]{1,0:T(8,128)S(1)} %bitcast.7, f32[1,256]{1,0:T(1,128)S(1)} %get-tuple-element.12.mass_ref), custom_call_target="tpu_custom_call" | custom-call | tf_op jit(solution)/shard_map/pallas_call | solution.py:201
  36.4 8.7 %all_to_all.35.parts_ref = f32[8,1,2304]{2,1,0:T(1,128)S(1)} all-to-all(f32[8,1,2304]{2,1,0:T(1,128)S(1)} %get-tuple-element.14), channel_id=1, replica_groups=mesh['y'=4,'x'=4,'core'=2,'z'=16] {'x','core'}, dimensions={0} | all-to-all | bytes 147456 | tf_op jit(solution)/shard_map/all_to_all | solution.py:212
  45.1 0.6 shard_map.62
  45.7 8.2 %all_to_all.36.parts_ref = f32[4,1,1024]{2,1,0:T(1,128)S(1)} all-to-all(f32[4,1,1024]{2,1,0:T(1,128)S(1)} %get-tuple-element.15), channel_id=1, replica_groups=mesh['y'=4,'x'=4,'core'=2,'z'=16] {'y'}, dimensions={0} | all-to-all | bytes 32768 | tf_op jit(solution)/shard_map/all_to_all | solution.py:212
  54.0 18.0 %all_to_all.37.parts_ref = f32[16,1,1024]{2,1,0:T(1,128)S(1)} all-to-all(f32[16,1,1024]{2,1,0:T(1,128)S(1)} %shard_map.63), channel_id=1, replica_groups=mesh['y'=4,'x'=4,'core'=2,'z'=16] {'z'}, dimensions={0} | all-to-all | bytes 131072 | tf_op jit(solution)/shard_map/all_to_all | solution.py:212
  72.0 0.0 copy-start.1
  72.0 0.7 shard_map.64
  72.7 11.0 %all_to_all.38.parts_ref = f32[8,1,2048]{2,1,0:T(1,128)S(1)} all-to-all(f32[8,1,2048]{2,1,0:T(1,128)S(1)} %shard_map.64), channel_id=1, replica_groups=mesh['y'=4,'x'=4,'core'=2,'z'=16] {'x','core'}, dimensions={0} | all-to-all | bytes 131072 | tf_op jit(solution)/shard_map/all_to_all | solution.py:212
  83.7 0.7 shard_map.65
  84.4 13.8 %all_to_all.39.landed_ref = f32[16,1,384]{2,1,0:T(1,128)S(1)} all-to-all(f32[16,1,384]{2,1,0:T(1,128)S(1)} %shard_map.65), channel_id=1, replica_groups=mesh['y'=4,'x'=4,'core'=2,'z'=16] {'z'}, dimensions={0} | all-to-all | bytes 49152 | tf_op jit(solution)/shard_map/all_to_all | solution.py:212
  98.2 12.1 %all_to_all.40.parts_ref = f32[32,1,128]{2,1,0:T(1,128)S(1)} all-to-all(f32[32,1,128]{2,1,0:T(1,128)S(1)} %shard_map.66), channel_id=1, replica_groups=mesh['y'=4,'x'=4,'core'=2,'z'=16] {'y','x','core'}, dimensions={0} | all-to-all | bytes 32768 | tf_op jit(solution)/shard_map/all_to_all | solution.py:212
  110.4 0.0 copy-done.1
  110.4 0.7 shard_map.67
  (2 shorter events, 0.0 us)
Async XLA Ops:
  2.2 31.6 %all-to-all-start = ((f32[16,1,3328]{2,1,0:T(1,128)}), f32[16,1,3328]{2,1,0:T(1,128)S(1)}, u32[]{:S(2)}, u32[]{:S(2)}) async-start(f32[16,1,3328]{2,1,0:T(1,128)} %bitcast.11), calls=%async_computation | async-start | bytes 425984 | tf_op jit(solution)/shard_map/all_to_all | solution.py:212
  32.8 0.7 copy-start
  72.0 38.4 %copy-start.1 = (f32[512]{0:T(512)S(1)}, f32[512]{0:T(512)}, u32[]{:S(2)}) copy-start(f32[512]{0:T(512)} %param.7) | copy-start | bytes 6148

commit v10 on v9

--- a/solution.py
+++ b/solution.py
@@ -15,6 +15,7 @@
 ROWS, COLS = 2048, 1024
 PIECE = 64
 OWN = 256
+DOWN = [-k % NZ for k in range(NZ)]
 ORDER = [(12 - k) % NZ for k in range(NZ)]
 EPS = 2.0
 FULL = 60 << 20
@@ -153,7 +154,7 @@
     own = scale_ref[:, pl.ds(pl.multiple_of(me * OWN, OWN), OWN)]
     for j in range(COLS // 128):
         total = columns(gibbs_ref, scale_ref, j)
-        for k in (ORDER[2 * j], ORDER[2 * j + 1]):
+        for k in (DOWN[ORDER[2 * j]], DOWN[ORDER[2 * j + 1]]):
             leaving_ref[k, :, 0:OWN] = own
             leaving_ref[k, :, OWN : OWN + 128] = total
             total = pltpu.roll(total, PIECE, 1)
@@ -184,7 +185,7 @@
 
 def potential_kernel(landed_ref, parts_ref, mass_ref, rows_ref, out_ref):
     for k in range(NZ):
-        rows_ref[k] = EPS * jnp.log(landed_ref[k, :, 0:OWN])
+        rows_ref[DOWN[k]] = EPS * jnp.log(landed_ref[k, :, 0:OWN])
     lane = lax.broadcasted_iota(jnp.int32, (1, 128), 1)
     for t in range(NG // 2):
         a, b = (sum(parts_ref[y * NG + g] for y in range(NY)) for g in (2 * t, 2 * t + 1))
@@ -248,7 +249,7 @@
     (leaving,) = call(
         last_column_kernel, (f32(NZ, 1, OWN + 128),), gibbs, swap(row_parts, GROUP), row_mass, scratch=(scale,)
     )
-    landed = swap(leaving, "z")
+    landed = swap(leaving, "z", [DOWN])
     (col_parts,) = call(landing_kernel, (f32(NY * NG, 1, 128),), landed)
     row_out, col_out = call(
         potential_kernel, (f32(NZ, 1, OWN), f32(NX, 128)), landed, swap(col_parts, PLANE), tgt_mass

time: 112 us -> 111 us (level)
  no operation moved by 1% of the time
where the time goes in v10:
time: 111 us
  blocking collectives  86.4 us (78%)
  starting transfers between devices  16 us (14%)
  Pallas kernels  7.15 us (6%)
    all_to_all x6, blocking collectives, swap(): lax.all_to_all(value, axes, 0, 0, tiled=True, axis_index_groups=groups)  71.7 us
    all_to_all x1, starting transfers between devices, swap(): lax.all_to_all(value, axes, 0, 0, tiled=True, axis_index_groups=groups)  16 us
    all_gather x1, blocking collectives, local(): lax.all_gather(src_cells, GROUP)  14.7 us
    pallas_call x9, Pallas kernels, call(): pl.pallas_call(kernel, out_shape=outs, in_specs=[pl.BlockSpec(memory_spac...  7.15 us
  transfers between devices with their start and end apart: 1, of which 0 were waited for; matrix products, arithmetic and copies ran while one was open for 0% of the time, Pallas kernels for 0%

profile of v10, /device:TPU:1, one launch (start us, length us, event | category | flops | bytes accessed | tf_op | source)
XLA Modules:
  0.0 110.9 jit_solution(9330700117615512476)
XLA Ops:
  0.6 1.5 %shard_map.60 = f32[416,128]{1,0:T(8,128)} custom-call(f32[50,512]{1,0:T(8,128)} %tgt_ref.1, f32[4,128]{1,0:T(4,128)} %bitcast.9), custom_call_target="tpu_custom_call" | custom-call | tf_op jit(solution)/shard_map/pallas_call | solution.py:202
  2.2 16.0 %all-to-all-start = ((f32[16,1,3328]{2,1,0:T(1,128)}), f32[16,1,3328]{2,1,0:T(1,128)S(1)}, u32[]{:S(2)}, u32[]{:S(2)}) async-start(f32[16,1,3328]{2,1,0:T(1,128)} %bitcast.11), calls=%async_computation | async-start | bytes 425984 | tf_op jit(solution)/shard_map/all_to_all | solution.py:213
  18.1 14.7 %all-gather.1.rows_ref = f32[8,50,256]{2,1,0:T(8,128)S(1)} all-gather(f32[1,50,256]{2,1,0:T(8,128)} %bitcast.12), channel_id=2, replica_groups=mesh['y'=4,'x'=4,'core'=2,'z'=16] {'x','core'}, dimensions={0}, use_global_device_ids=true | all-gather | bytes 460800 | tf_op jit(solution)/shard_map/all_gather | solution.py:231
  32.8 0.0 copy-start
  32.8 0.7 copy-done
  33.5 0.2 shard_map.59
  33.7 0.0 all-to-all-done
  33.8 2.7 %shard_map.61 = (f32[1024,2048]{1,0:T(8,128)S(1)}, f32[8,1,2304]{2,1,0:T(1,128)S(1)}, f32[1,1024]{1,0:T(1,128)S(1)}) custom-call(bf16[384,2048]{1,0:T(8,128)(2,1)S(1)} %get-tuple-element.11.x_ref, f32[416,128]{1,0:T(8,128)S(1)} %bitcast.7, f32[1,256]{1,0:T(1,128)S(1)} %get-tuple-element.12.mass_ref), custom_call_target="tpu_custom_call" | custom-call | tf_op jit(solution)/shard_map/pallas_call | solution.py:202
  36.4 8.7 %all_to_all.35.parts_ref = f32[8,1,2304]{2,1,0:T(1,128)S(1)} all-to-all(f32[8,1,2304]{2,1,0:T(1,128)S(1)} %get-tuple-element.14), channel_id=1, replica_groups=mesh['y'=4,'x'=4,'core'=2,'z'=16] {'x','core'}, dimensions={0} | all-to-all | bytes 147456 | tf_op jit(solution)/shard_map/all_to_all | solution.py:213
  45.1 0.6 shard_map.62
  45.7 8.2 %all_to_all.36.parts_ref = f32[4,1,1024]{2,1,0:T(1,128)S(1)} all-to-all(f32[4,1,1024]{2,1,0:T(1,128)S(1)} %get-tuple-element.15), channel_id=1, replica_groups=mesh['y'=4,'x'=4,'core'=2,'z'=16] {'y'}, dimensions={0} | all-to-all | bytes 32768 | tf_op jit(solution)/shard_map/all_to_all | solution.py:213
  54.0 18.0 %all_to_all.37.parts_ref = f32[16,1,1024]{2,1,0:T(1,128)S(1)} all-to-all(f32[16,1,1024]{2,1,0:T(1,128)S(1)} %shard_map.63), channel_id=1, replica_groups=mesh['y'=4,'x'=4,'core'=2,'z'=16] {'z'}, dimensions={0} | all-to-all | bytes 131072 | tf_op jit(solution)/shard_map/all_to_all | solution.py:213
  72.0 0.0 copy-start.1
  72.0 0.7 shard_map.64
  72.7 11.0 %all_to_all.38.parts_ref = f32[8,1,2048]{2,1,0:T(1,128)S(1)} all-to-all(f32[8,1,2048]{2,1,0:T(1,128)S(1)} %shard_map.64), channel_id=1, replica_groups=mesh['y'=4,'x'=4,'core'=2,'z'=16] {'x','core'}, dimensions={0} | all-to-all | bytes 131072 | tf_op jit(solution)/shard_map/all_to_all | solution.py:213
  83.7 0.7 shard_map.65
  84.4 13.8 %all_to_all.39.landed_ref = f32[16,1,384]{2,1,0:T(1,128)S(1)} all-to-all(f32[16,1,384]{2,1,0:T(1,128)S(1)} %shard_map.65), channel_id=1, replica_groups={{0,15,14,13,12,11,10,9,8,7,6,5,4,3,2,1},{16,31,30,29,28,27,26,25,24,23,..., dimensions={0} | all-to-all | bytes 49152 | tf_op jit(solution)/shard_map/all_to_all | solution.py:213
  98.2 12.0 %all_to_all.40.parts_ref = f32[32,1,128]{2,1,0:T(1,128)S(1)} all-to-all(f32[32,1,128]{2,1,0:T(1,128)S(1)} %shard_map.66), channel_id=1, replica_groups=mesh['y'=4,'x'=4,'core'=2,'z'=16] {'y','x','core'}, dimensions={0} | all-to-all | bytes 32768 | tf_op jit(solution)/shard_map/all_to_all | solution.py:213
  110.2 0.0 copy-done.1
  110.2 0.7 shard_map.67
  (2 shorter events, 0.0 us)
Async XLA Ops:
  2.2 31.6 %all-to-all-start = ((f32[16,1,3328]{2,1,0:T(1,128)}), f32[16,1,3328]{2,1,0:T(1,128)S(1)}, u32[]{:S(2)}, u32[]{:S(2)}) async-start(f32[16,1,3328]{2,1,0:T(1,128)} %bitcast.11), calls=%async_computation | async-start | bytes 425984 | tf_op jit(solution)/shard_map/all_to_all | solution.py:213
  32.8 0.7 copy-start
  72.0 38.2 %copy-start.1 = (f32[512]{0:T(512)S(1)}, f32[512]{0:T(512)}, u32[]{:S(2)}) copy-start(f32[512]{0:T(512)} %param.7) | copy-start | bytes 6148
